TPU v7x, 128 devices: a whole 4x4x4 slice. The times are simulated.
128 devices in a mesh: expert: 32 (over z, x, core), tensor: 4 (over y).
Axes of the slice: x: 4, y: 4, z: 4, core: 2. Of those that a mesh axis runs over, the one named last changes fastest.
Arguments:
- tokens: bfloat16 [16384, 2560], P(('expert', 'tensor')), may hold values from -6 to 6
- expert_ids: int32 [16384, 1], P(('expert', 'tensor')), may hold values from 0 to 31; in each aligned block of 128 rows (0 to 127, 128 to 255, ...) at most 6 rows name the same one
- live_counts: int32 [128], P(('expert', 'tensor')), may hold values from 1 to 128, 10240 in all
- router: bfloat16 [2560, 32], replicated, may hold values from -0.125 to 0.125
- up_weight: bfloat16 [32, 2560, 4096], P('expert', None, 'tensor'), may hold values from -0.125 to 0.125
- down_weight: bfloat16 [32, 4096, 2560], P('expert', 'tensor'), may hold values from -0.09375 to 0.09375
- out_grad: bfloat16 [16384, 2560], P(('expert', 'tensor')), may hold values from -6 to 6
Outputs:
- mixed: bfloat16 [16384, 2560], P(('expert', 'tensor'))
- token_grad: bfloat16 [16384, 2560], P(('expert', 'tensor'))
- up_grad: bfloat16 [32, 2560, 4096], P('expert', None, 'tensor')
- down_grad: bfloat16 [32, 4096, 2560], P('expert', 'tensor')
- router_grad: float32 [2560, 32], replicated
Inputs may be any that keep to these rules, and one draw needn't show every extreme that they name: `expert_ids`: within the rows of one device (aligned blocks of 128 rows) no expert is named by more than 6 rows; in every draw some expert is named by exactly 6 rows of some device. live_counts[k] real token rows lead device k's 128 rows, the rest are padding; some device holds exactly 128 real rows in every draw.
All inputs are finite; a program needn't handle non-finite values.
Results may differ from a plain program's by a relative error of at most 0.0063.
Values may be sent and summed in bfloat16 or wider, within the bound.
A program may use at most 128 MiB of HBM per device.

v0:
```python
import jax
import jax.numpy as jnp
from jax import lax
from jax.sharding import PartitionSpec as P


def silu_slope(hidden):
    sig = jax.nn.sigmoid(hidden)
    return sig * (1.0 + hidden * (1.0 - sig))


def local_work(rows, cot_rows, w_up, w_down):
    hidden = jnp.dot(rows, w_up, preferred_element_type=jnp.float32)
    active = jax.nn.silu(hidden).astype(jnp.bfloat16)
    hidden_cot = (
        lax.dot_general(
            cot_rows, w_down, (((1,), (1,)), ((), ())), preferred_element_type=jnp.float32
        )
        * silu_slope(hidden)
    ).astype(jnp.bfloat16)
    down_grad = lax.dot_general(
        active, cot_rows, (((0,), (0,)), ((), ())), preferred_element_type=jnp.float32
    ).astype(jnp.bfloat16)[None]
    up_grad = lax.dot_general(
        rows, hidden_cot, (((0,), (0,)), ((), ())), preferred_element_type=jnp.float32
    ).astype(jnp.bfloat16)[None]
    return (active, hidden_cot, down_grad, up_grad)


def widen_copies(box, experts, groups, most, width):
    return jnp.broadcast_to(box[:, None], (experts, groups, most, width)).reshape(
        experts * groups, most, width
    )


def fold_copies(back, experts, groups, most, width):
    return jnp.sum(back.reshape(experts, groups, most, width), axis=1).astype(jnp.bfloat16)


def back_product(hidden_cot, w_up):
    return lax.dot_general(
        hidden_cot, w_up, (((1,), (1,)), ((), ())), preferred_element_type=jnp.float32
    )


def per_device(tokens, expert_ids, live_counts, router, up_weight, down_weight, out_grad):
    tok_rows, width = tokens.shape
    experts = router.shape[1]
    most = 3 * tok_rows // (2 * experts)
    groups = lax.axis_size("tensor")
    slots = experts * most
    ids = expert_ids[:, 0]
    live = lax.iota(jnp.int32, tok_rows) < live_counts[0]
    live_rows = jnp.where(live[:, None], tokens, jnp.zeros_like(tokens))
    chosen = ids[:, None] == lax.iota(jnp.int32, experts)[None, :]
    chosen_int = chosen.astype(jnp.int32)
    onehot = chosen.astype(jnp.float32)
    logits = jnp.dot(tokens, router, preferred_element_type=jnp.float32)
    gate = jax.nn.sigmoid(jnp.sum(logits * onehot, axis=1))
    rank = jnp.sum(jnp.cumsum(chosen_int, axis=0) * chosen_int, axis=1) - 1
    target = ids * most + rank
    placing = (lax.iota(jnp.int32, slots)[:, None] == target[None, :]).astype(jnp.bfloat16)
    w_up = up_weight[0]
    w_down = down_weight[0]
    outbox = (
        jnp.dot(placing, live_rows, preferred_element_type=jnp.float32)
        .astype(jnp.bfloat16)
        .reshape(experts, most, width)
    )
    out_cot = jnp.where(live[:, None], gate[:, None] * out_grad.astype(jnp.float32), 0.0).astype(
        jnp.bfloat16
    )
    cot_box = (
        jnp.dot(placing, out_cot, preferred_element_type=jnp.float32)
        .astype(jnp.bfloat16)
        .reshape(experts, most, width)
    )
    inbox = lax.all_to_all(
        widen_copies(outbox, experts, groups, most, width),
        ("expert", "tensor"),
        split_axis=0,
        concat_axis=0,
        tiled=True,
    )
    rows = inbox.reshape(-1, width)
    hidden = jnp.dot(rows, w_up, preferred_element_type=jnp.float32)
    active = jax.nn.silu(hidden).astype(jnp.bfloat16)
    partial_value = jnp.dot(active, w_down, preferred_element_type=jnp.float32).reshape(
        experts * groups, most, width
    )
    returned = lax.all_to_all(
        partial_value, ("expert", "tensor"), split_axis=0, concat_axis=0, tiled=True
    )
    expert_out = fold_copies(returned, experts, groups, most, width)
    cot_inbox = lax.all_to_all(
        widen_copies(cot_box, experts, groups, most, width),
        ("expert", "tensor"),
        split_axis=0,
        concat_axis=0,
        tiled=True,
    )
    cot_rows = cot_inbox.reshape(-1, width)
    active, hidden_cot, down_grad, up_grad = local_work(rows, cot_rows, w_up, w_down)
    token_part = back_product(hidden_cot, w_up).reshape(experts * groups, most, width)
    token_back = lax.all_to_all(
        token_part, ("expert", "tensor"), split_axis=0, concat_axis=0, tiled=True
    )
    expert_cot = fold_copies(token_back, experts, groups, most, width)
    out_rows = lax.dot_general(
        placing,
        expert_out.reshape(slots, width),
        (((0,), (0,)), ((), ())),
        preferred_element_type=jnp.float32,
    ).astype(jnp.bfloat16)
    mixed = (gate[:, None] * out_rows.astype(jnp.float32)).astype(jnp.bfloat16)
    slope = (
        jnp.sum(out_grad.astype(jnp.float32) * out_rows.astype(jnp.float32), axis=1)
        * gate
        * (1.0 - gate)
    )
    cot_tokens = lax.dot_general(
        placing,
        expert_cot.reshape(slots, width),
        (((0,), (0,)), ((), ())),
        preferred_element_type=jnp.float32,
    ).astype(jnp.bfloat16)
    columns = lax.dot_general(
        chosen.astype(jnp.bfloat16),
        router,
        (((1,), (1,)), ((), ())),
        preferred_element_type=jnp.float32,
    )
    token_grad = (cot_tokens.astype(jnp.float32) + slope[:, None] * columns).astype(jnp.bfloat16)
    router_local = lax.dot_general(
        live_rows.astype(jnp.float32),
        slope[:, None] * onehot,
        (((0,), (0,)), ((), ())),
        precision=lax.Precision.HIGHEST,
    )
    router_grad = lax.psum(router_local, ("expert", "tensor"))
    return (mixed, token_grad, up_grad, down_grad, router_grad)


def solution(mesh):
    in_specs = (
        P(("expert", "tensor"), None),
        P(("expert", "tensor"), None),
        P(("expert", "tensor")),
        P(),
        P("expert", None, "tensor"),
        P("expert", "tensor", None),
        P(("expert", "tensor"), None),
    )
    out_specs = (
        P(("expert", "tensor"), None),
        P(("expert", "tensor"), None),
        P("expert", None, "tensor"),
        P("expert", "tensor", None),
        P(),
    )
    return jax.shard_map(
        per_device, mesh=mesh, in_specs=in_specs, out_specs=out_specs, check_vma=False
    )
```

profile of v0, /device:TPU:1, one launch (start us, length us, event | category | flops | bytes accessed | tf_op | source)
XLA Modules:
  0.0 639.2 jit_solution(9002522458645514613)
XLA Ops:
  7.9 0.7 fusion.32
  8.9 0.7 select_reduce_fusion
  9.6 0.7 add_add_fusion
  10.2 1.6 convolution_convert_fusion.3
  12.6 75.6 %all_to_all.20 = bf16[128,6,2560]{2,1,0:T(8,128)(2,1)} all-to-all(bf16[128,6,2560]{2,1,0:T(8,128)(2,1)S(1)} %bitcast.41), channel_id=1, replica_groups=mesh['expert'=32,'tensor'=4] {'expert','tensor'}, dimensions={0} | all-to-all | bytes 7864320 | tf_op jit(solution)/shard_map/all_to_all | solution.py:78
  88.2 7.2 %reshape.67 = bf16[768,2560]{1,0:T(8,128)(2,1)} reshape(bf16[128,6,2560]{2,1,0:T(8,128)(2,1)} %all_to_all.20) | data formatting | bytes 7864320 | tf_op jit(solution)/shard_map/reshape | solution.py:85
  95.4 10.4 %multiply_convert_fusion.1 = (bf16[768,1024]{1,0:T(8,128)(2,1)}, f32[768,1024]{1,0:T(8,128)}) fusion(bf16[768,2560]{1,0:T(8,128)(2,1)} %reshape.67, bf16[1,2560,1024]{2,1,0:T(8,128)(2,1)} %param.11), kind=kOutput, calls=%fused_computation.24 | convolution fusion | flops 4030464000 | bytes 13893632 | tf_op jit(solution)/shard_map/dot_general | solution.py:86
  105.8 2.5 dot_general.47
  108.3 8.8 %fusion.2 = f32[128,6,2560]{2,0,1:T(8,128)S(1)} fusion(bf16[1,1024,2560]{2,1,0:T(8,128)(2,1)} %param.12, bf16[128,6,1024]{2,1,0:T(8,128)(2,1)S(1)} %dot_general.47), kind=kOutput, calls=%fused_computation.6 | convolution fusion | flops 4026531840 | bytes 14680064 | tf_op jit(solution)/shard_map/dot_general | solution.py:88
  117.2 8.6 %copy.23 = f32[128,6,2560]{2,1,0:T(8,128)} copy(f32[128,6,2560]{2,0,1:T(8,128)S(1)} %fusion.2) | data formatting | bytes 15728640 | tf_op jit(solution)/shard_map/dot_general | solution.py:88
  125.7 16.5 %all-to-all-start.1 = ((f32[128,6,2560]{2,1,0:T(8,128)}), f32[128,6,2560]{2,1,0:T(8,128)}, u32[]{:S(2)}, u32[]{:S(2)}) async-start(f32[128,6,2560]{2,1,0:T(8,128)} %copy.23), calls=%async_computation.1 | async-start | bytes 20971520 | tf_op jit(solution)/shard_map/all_to_all | solution.py:91
  142.6 129.3 %all-to-all-done.1 = f32[128,6,2560]{2,1,0:T(8,128)} async-done(((f32[128,6,2560]{2,1,0:T(8,128)}), f32[128,6,2560]{2,1,0:T(8,128)}, u32[]{:S(2)}, u32[]{:S(2)}) %all-to-all-start.1) | async-done | bytes 7864352 | tf_op jit(solution)/shard_map/all_to_all | solution.py:91
  271.9 5.2 bitcast_reduce_fusion.1
  278.3 1.6 fusion.20
  279.9 2.6 convolution_convert_fusion.2
  282.4 1.4 broadcast_in_dim.55
  284.2 67.8 %all_to_all.21 = bf16[128,6,2560]{2,1,0:T(8,128)(2,1)} all-to-all(bf16[128,6,2560]{2,1,0:T(8,128)(2,1)S(1)} %bitcast.42), channel_id=1, replica_groups=mesh['expert'=32,'tensor'=4] {'expert','tensor'}, dimensions={0} | all-to-all | bytes 7864320 | tf_op jit(solution)/shard_map/all_to_all | solution.py:95
  352.0 7.2 %reshape.70 = bf16[768,2560]{1,0:T(8,128)(2,1)} reshape(bf16[128,6,2560]{2,1,0:T(8,128)(2,1)} %all_to_all.21) | data formatting | bytes 7864320 | tf_op jit(solution)/shard_map/reshape | solution.py:102
  359.3 10.5 %multiply_convert_fusion = bf16[768,1024]{1,0:T(8,128)(2,1)} fusion(f32[768,1024]{1,0:T(8,128)} %get-tuple-element.8, bf16[768,2560]{1,0:T(8,128)(2,1)} %reshape.70, bf16[1,1024,2560]{2,1,0:T(8,128)(2,1)} %param.12), kind=kOutput, calls=%fused_computation.23 | convolution fusion | flops 4033609728 | bytes 13893632 | tf_op jit(solution)/shard_map/dot_general | solution.py:16
  369.7 3.7 dot_general.52
  373.4 9.6 %fusion = f32[128,6,2560]{2,0,1:T(8,128)S(1)} fusion(bf16[1,2560,1024]{2,1,0:T(8,128)(2,1)} %param.11, bf16[128,6,1024]{2,1,0:T(8,128)(2,1)} %dot_general.52), kind=kOutput, calls=%fused_computation.4 | convolution fusion | flops 4026531840 | bytes 14680064 | tf_op jit(solution)/shard_map/dot_general | solution.py:41
  383.0 8.6 %copy.27 = f32[128,6,2560]{2,1,0:T(8,128)} copy(f32[128,6,2560]{2,0,1:T(8,128)S(1)} %fusion) | data formatting | bytes 15728640 | tf_op jit(solution)/shard_map/dot_general | solution.py:41
  391.5 5.0 all-to-all-start.3
  396.8 1.2 fusion.26
  398.0 1.0 multiply_convert_fusion.2
  399.0 9.4 %fusion.9 = bf16[1,1024,2560]{2,1,0:T(8,128)(2,1)} fusion(bf16[768,1024]{1,0:T(8,128)(2,1)} %get-tuple-element.7, bf16[768,2560]{1,0:T(8,128)(2,1)} %reshape.70), kind=kOutput, calls=%fused_computation.13 | convolution fusion | flops 4029153280 | bytes 10747904 | tf_op jit(solution)/shard_map/dot_general | solution.py:21
  408.4 6.0 fusion.8
  414.4 110.6 %all-to-all-done.3 = f32[128,6,2560]{2,1,0:T(8,128)} async-done(((f32[128,6,2560]{2,1,0:T(8,128)}), f32[128,6,2560]{2,1,0:T(8,128)}, u32[]{:S(2)}, u32[]{:S(2)}) %all-to-all-start.3) | async-done | bytes 7864352 | tf_op jit(solution)/shard_map/all_to_all | solution.py:105
  525.0 5.2 bitcast_reduce_fusion
  531.8 1.2 fusion.11
  533.1 97.2 %all-reduce.2.cloned.1.call-done = f32[2560,32]{0,1:T(8,128)} async-done(((f32[2560,32]{0,1:T(8,128)}), f32[2560,32]{0,1:T(8,128)}) %all-reduce.2.cloned.1.call-update) | async-done | bytes 327696 | tf_op jit(solution)/shard_map/psum | solution.py:140
  630.2 1.7 copy.42
  (28 shorter events, 4.9 us)
Async XLA Ops:
  7.2 135.1 %copy-start = (bf16[2560,32]{0,1:T(8,128)(2,1)S(1)}, bf16[2560,32]{0,1:T(8,128)(2,1)}, u32[]{:S(2)}) copy-start(bf16[2560,32]{0,1:T(8,128)(2,1)} %param.10) | copy-start | bytes 491524
  125.7 16.5 %copy-start.1 = (bf16[128,2560]{1,0:T(8,128)(2,1)S(1)}, bf16[128,2560]{1,0:T(8,128)(2,1)}, u32[]{:S(2)}) copy-start(bf16[128,2560]{1,0:T(8,128)(2,1)} %param.7) | copy-start | bytes 1966084
  125.7 16.5 %copy-start.4 = (s32[128,1]{0,1:T(1,128)S(1)}, s32[128,1]{0,1:T(1,128)}, u32[]{:S(2)}) copy-start(s32[128,1]{0,1:T(1,128)} %param.8) | copy-start | bytes 1540
  125.7 146.2 %all-to-all-start.1 = ((f32[128,6,2560]{2,1,0:T(8,128)}), f32[128,6,2560]{2,1,0:T(8,128)}, u32[]{:S(2)}, u32[]{:S(2)}) async-start(f32[128,6,2560]{2,1,0:T(8,128)} %copy.23), calls=%async_computation.1 | async-start | bytes 20971520 | tf_op jit(solution)/shard_map/all_to_all | solution.py:91
  391.5 133.5 %all-to-all-start.3 = ((f32[128,6,2560]{2,1,0:T(8,128)}), f32[128,6,2560]{2,1,0:T(8,128)}, u32[]{:S(2)}, u32[]{:S(2)}) async-start(f32[128,6,2560]{2,1,0:T(8,128)} %copy.27), calls=%async_computation.3 | async-start | bytes 20971520 | tf_op jit(solution)/shard_map/all_to_all | solution.py:105
  396.6 233.7 %all-reduce.2.cloned.1.call-start = ((), (), s32[]{:S(2)}) async-start(), calls=%async_computation.4 | async-start | bytes 655360 | tf_op jit(solution)/shard_map/psum | solution.py:140
  399.0 9.4 %copy-start.2 = (bf16[768,2560]{1,0:T(8,128)(2,1)S(1)}, bf16[768,2560]{1,0:T(8,128)(2,1)}, u32[]{:S(2)}) copy-start(bf16[768,2560]{1,0:T(8,128)(2,1)} %reshape.67) | copy-start | bytes 11796484
  399.0 9.4 %copy-start.3 = (bf16[768,1024]{1,0:T(8,128)(2,1)S(1)}, bf16[768,1024]{1,0:T(8,128)(2,1)}, u32[]{:S(2)}) copy-start(bf16[768,1024]{1,0:T(8,128)(2,1)} %multiply_convert_fusion) | copy-start | bytes 4718596
Sparse Core Ops, SparseCore 0:
  402.7 227.4 all-reduce.1
where the time goes:
time: 650 us; the launch traced here: 639 us
  waiting for transfers between devices  337 us (52%)
  blocking collectives  143 us (22%)
  matrix products  63.5 us (10%)
  local copies, waits for them, and re-layouts  44.5 us (7%)
  starting transfers between devices  21.8 us (3%)
  between operations  15.3 us (2%)
  other arithmetic  13.5 us (2%)
    all_to_all x1, waiting for transfers between devices, per_device(): lax.all_to_all(partial_value, ('expert', 'tensor'), split_axis=0, concat_...  129 us
    all_to_all x1, waiting for transfers between devices, per_device(): lax.all_to_all(token_part, ('expert', 'tensor'), split_axis=0, concat_axi...  111 us
    psum x1, waiting for transfers between devices, per_device(): router_grad = lax.psum(router_local, ('expert', 'tensor'))  97.2 us
    all_to_all x1, blocking collectives, per_device(): lax.all_to_all(widen_copies(outbox, experts, groups, most, width), ('expe...  75.6 us
    all_to_all x1, blocking collectives, per_device(): lax.all_to_all(widen_copies(cot_box, experts, groups, most, width), ('exp...  67.8 us
    all_to_all x1, starting transfers between devices, per_device(): lax.all_to_all(partial_value, ('expert', 'tensor'), split_axis=0, concat_...  16.5 us
  transfers between devices with their start and end apart: 3, of which 3 were waited for; matrix products, arithmetic and copies ran while one was open for 4% of the time, Pallas kernels for 0%

commit v1 on v0

v1 whole, which is shorter than its diff:
```python
import jax
import jax.numpy as jnp
from jax import lax
from jax.sharding import PartitionSpec as P

F32, BF16 = jnp.float32, jnp.bfloat16


def per_device(tokens, expert_ids, live_counts, router, up_weight, down_weight, out_grad):
    tok_rows, width = tokens.shape
    experts = router.shape[1]
    most = 3 * tok_rows // (2 * experts)
    slots = experts * most
    ids = expert_ids[:, 0]
    live = lax.iota(jnp.int32, tok_rows) < live_counts[0]
    chosen = ids[:, None] == lax.iota(jnp.int32, experts)[None, :]
    logits = jnp.dot(tokens, router, preferred_element_type=F32)
    gate = jax.nn.sigmoid(jnp.sum(jnp.where(chosen, logits, 0.0), axis=1))
    before = (lax.iota(jnp.int32, tok_rows)[:, None] > lax.iota(jnp.int32, tok_rows)[None, :])
    same = ids[:, None] == ids[None, :]
    rank = jnp.sum(jnp.where(before & same, 1, 0), axis=1)
    target = jnp.where(live, ids * most + rank, -1)
    placing = (lax.iota(jnp.int32, slots)[:, None] == target[None, :]).astype(BF16)
    w_up = up_weight[0]
    w_down = down_weight[0]
    out_cot = (gate[:, None] * out_grad.astype(F32)).astype(BF16)
    both = jnp.concatenate([tokens, out_cot], axis=1)
    box = jnp.dot(placing, both, preferred_element_type=F32).astype(BF16)
    inbox = lax.all_to_all(
        box.reshape(experts, most, 2 * width), "expert", split_axis=0, concat_axis=0, tiled=True
    ).reshape(slots, 2 * width)
    rows_all = lax.all_gather(inbox, "tensor", axis=0, tiled=True)
    rows, cot = rows_all[:, :width], rows_all[:, width:]
    me = lax.axis_index("expert")
    column = lax.dynamic_index_in_dim(router, me, axis=1, keepdims=False)
    slot_logit = jnp.dot(rows, router, preferred_element_type=F32)
    slot_gate = jax.nn.sigmoid(lax.dynamic_index_in_dim(slot_logit, me, axis=1, keepdims=False))
    hidden = jnp.dot(rows, w_up, preferred_element_type=F32)
    sig = jax.nn.sigmoid(hidden)
    active = (hidden * sig).astype(BF16)
    back = lax.dot_general(cot, w_down, (((1,), (1,)), ((), ())), preferred_element_type=F32)
    hidden_cot = (back * (sig * (1.0 + hidden * (1.0 - sig)))).astype(BF16)
    slope = jnp.sum(active.astype(F32) * back, axis=1) * (1.0 - slot_gate)
    tn = (((0,), (0,)), ((), ()))
    down_grad = lax.dot_general(active, cot, tn, preferred_element_type=F32).astype(BF16)[None]
    up_grad = lax.dot_general(rows, hidden_cot, tn, preferred_element_type=F32).astype(BF16)[None]
    value = jnp.dot(active, w_down, preferred_element_type=F32).astype(BF16)
    grad = (
        lax.dot_general(hidden_cot, w_up, (((1,), (1,)), ((), ())), preferred_element_type=F32)
        + slope[:, None] * column.astype(F32)[None, :]
    ).astype(BF16)
    router_col = jnp.sum(rows.astype(F32) * slope[:, None], axis=0)
    router_col = lax.psum(router_col, "tensor")
    router_grad = lax.all_gather(router_col, "expert", axis=0).T
    summed = lax.psum_scatter(
        jnp.concatenate([value, grad], axis=1), "tensor", scatter_dimension=0, tiled=True
    )
    back_box = lax.all_to_all(
        summed.reshape(experts, most, 2 * width), "expert", split_axis=0, concat_axis=0, tiled=True
    ).reshape(slots, 2 * width)
    out = lax.dot_general(placing, back_box, tn, preferred_element_type=F32)
    mixed = (gate[:, None] * out[:, :width]).astype(BF16)
    token_grad = out[:, width:].astype(BF16)
    return (mixed, token_grad, up_grad, down_grad, router_grad)


def solution(mesh):
    rows = P(("expert", "tensor"), None)
    in_specs = (
        rows,
        rows,
        P(("expert", "tensor")),
        P(),
        P("expert", None, "tensor"),
        P("expert", "tensor", None),
        rows,
    )
    out_specs = (rows, rows, P("expert", None, "tensor"), P("expert", "tensor", None), P())
    return jax.shard_map(
        per_device, mesh=mesh, in_specs=in_specs, out_specs=out_specs, check_vma=False
    )
```

time: 650 us -> 319 us (0.49); the launches traced: 639 us -> 317 us
  waiting for transfers between devices: 337 us -> 125 us
  blocking collectives: 143 us -> 85.3 us
  local copies, waits for them, and re-layouts: 44.5 us -> 14.7 us
  starting transfers between devices: 21.8 us -> 7.84 us
  matrix products: 63.5 us -> 55.6 us
    all_to_all x2 -> x1, waiting for transfers between devices: 240 us -> 16.3 us  [per_device(): lax.all_to_all(summed.reshape(experts, most, 2 * width), 'expert', split_...]
    all_to_all x2 -> x1, blocking collectives: 143 us -> 43.2 us  [per_device(): lax.all_to_all(box.reshape(experts, most, 2 * width), 'expert', split_axi...]
    psum x1 -> x0, waiting for transfers between devices: 97.2 us -> none  [per_device(): router_grad = lax.psum(router_local, ('expert', 'tensor'))]
    all_gather x0 -> x1, waiting for transfers between devices: none -> 76.2 us  [per_device(): rows_all = lax.all_gather(inbox, 'tensor', axis=0, tiled=True)]
    reduce_scatter x0 -> x1, waiting for transfers between devices: none -> 32.3 us  [per_device(): lax.psum_scatter(jnp.concatenate([value, grad], axis=1), 'tensor', scatte...]
    all_gather x0 -> x1, blocking collectives: none -> 29.3 us  [per_device(): router_grad = lax.all_gather(router_col, 'expert', axis=0).T]
    dot_general x4 -> x0, local copies, waits for them, and re-layouts: 23.2 us -> none  [the longest x2 12.2 us: back_product(): lax.dot_general(hidden_cot, w_up, (((1,), (1,)), ((), ())), preferred_ele...]
    all_to_all x2 -> x1, starting transfers between devices: 21.5 us -> 7.76 us  [per_device(): lax.all_to_all(summed.reshape(experts, most, 2 * width), 'expert', split_...]
  transfers between devices with their start and end apart: 3 -> 3, of which waited for: 3 -> 3; matrix products, arithmetic and copies ran while one was open for 4% -> 7% of each run, Pallas kernels for 0% -> 0%
where the time goes in v1:
time: 319 us; the launch traced here: 317 us
  waiting for transfers between devices  125 us (39%)
  blocking collectives  85.3 us (27%)
  matrix products  55.6 us (17%)
  between operations  14.9 us (5%)
  local copies, waits for them, and re-layouts  14.7 us (5%)
  other arithmetic  14.2 us (4%)
  starting transfers between devices  7.84 us (2%)
    all_gather x1, waiting for transfers between devices, per_device(): rows_all = lax.all_gather(inbox, 'tensor', axis=0, tiled=True)  76.2 us
    all_to_all x1, blocking collectives, per_device(): lax.all_to_all(box.reshape(experts, most, 2 * width), 'expert', split_axi...  43.2 us
    reduce_scatter x1, waiting for transfers between devices, per_device(): lax.psum_scatter(jnp.concatenate([value, grad], axis=1), 'tensor', scatte...  32.3 us
    all_gather x1, blocking collectives, per_device(): router_grad = lax.all_gather(router_col, 'expert', axis=0).T  29.3 us
    all_to_all x1, waiting for transfers between devices, per_device(): lax.all_to_all(summed.reshape(experts, most, 2 * width), 'expert', split_...  16.3 us
    psum x1, blocking collectives, per_device(): router_col = lax.psum(router_col, 'tensor')  12.7 us
    dot_general x1, matrix products, per_device(): value = jnp.dot(active, w_down, preferred_element_type=F32).astype(BF16)  9.45 us
    dot_general x1, matrix products, per_device(): lax.dot_general(rows, hidden_cot, tn, preferred_element_type=F32)  9.39 us
  transfers between devices with their start and end apart: 3, of which 3 were waited for; matrix products, arithmetic and copies ran while one was open for 7% of the time, Pallas kernels for 0%

profile of v1, /device:TPU:1, one launch (start us, length us, event | category | flops | bytes accessed | tf_op | source)
XLA Modules:
  0.0 317.4 jit_solution(329693662515393767)
XLA Ops:
  7.2 0.0 all-gather.3.cloned.1.call-start
  7.9 0.9 select_reduce_fusion
  8.8 1.5 fusion.22
  10.3 0.7 compare_select_fusion
  11.0 1.3 multiply_convert_fusion.2
  12.2 3.0 convolution_convert_fusion
  15.2 2.6 reshape.50
  17.9 43.2 %all_to_all.10 = bf16[32,6,5120]{2,1,0:T(8,128)(2,1)} all-to-all(bf16[32,6,5120]{2,1,0:T(8,128)(2,1)S(1)} %reshape.50), channel_id=1, replica_groups=mesh['expert'=32,'tensor'=4] {'expert'}, dimensions={0} | all-to-all | bytes 3932160 | tf_op jit(solution)/shard_map/all_to_all | solution.py:29
  61.1 4.2 %reshape.51 = bf16[192,5120]{1,0:T(8,128)(2,1)} reshape(bf16[32,6,5120]{2,1,0:T(8,128)(2,1)} %all_to_all.10) | data formatting | bytes 3932160 | tf_op jit(solution)/shard_map/reshape | solution.py:31
  65.3 0.0 reduce-scatter.2.cloned.1.call-start
  65.4 76.2 %all-gather.3.cloned.1.call-done = bf16[768,5120]{1,0:T(8,128)(2,1)} async-done(((bf16[192,5120]{1,0:T(8,128)(2,1)}), bf16[768,5120]{1,0:T(8,128)(2,1)}) %all-gather.3.cloned.1.call-update) | async-done | bytes 7864336 | tf_op jit(solution)/shard_map/all_gather | solution.py:32
  141.6 7.3 %fusion.5 = f32[768,1024]{1,0:T(8,128)S(1)} fusion(bf16[1,2560,1024]{2,1,0:T(8,128)(2,1)} %param.11, bf16[768,5120]{1,0:T(8,128)(2,1)} %all-gather.3.cloned.1.call-done), kind=kOutput, calls=%fused_computation.11 | convolution fusion | flops 4026531840 | bytes 12320768 | tf_op jit(solution)/shard_map/dot_general | solution.py:38
  149.0 9.4 %fusion.7 = bf16[768,2560]{1,0:T(8,128)(2,1)} fusion(bf16[1,1024,2560]{2,1,0:T(8,128)(2,1)} %param.12, f32[768,1024]{1,0:T(8,128)S(1)} %fusion.5), kind=kOutput, calls=%fused_computation.13 | convolution fusion | flops 4032430080 | bytes 12320768 | tf_op jit(solution)/shard_map/dot_general | solution.py:47
  158.4 1.3 fusion.15
  159.7 0.0 slice-start.1
  159.7 7.5 %multiply_reduce_fusion.1 = (f32[768]{0:T(1024)S(1)}, bf16[768,1024]{1,0:T(8,128)(2,1)S(1)}) fusion(f32[768,1024]{1,0:T(8,128)S(1)} %fusion.5, bf16[1,1024,2560]{2,1,0:T(8,128)(2,1)} %param.12, bf16[768,5120]{1,0:T(8,128)(2,1)S(1)} %copy-done), kind=kOutput, calls=%fused_computation.18 | convolution fusion | flops 4037541120 | bytes 13896704 | tf_op jit(solution)/shard_map/dot_general | solution.py:41
  167.4 5.8 %add_convert_fusion = bf16[768,2560]{1,0:T(8,128)(2,1)} fusion(bf16[768,1024]{1,0:T(8,128)(2,1)S(1)} %get-tuple-element.6, bf16[1,2560,1024]{2,1,0:T(8,128)(2,1)S(1)} %bitcast.39, f32[2560]{0:T(1024)S(1)} %convert_reduce_fusion, f32[768]{0:T(1024)S(1)} %multiply_reduce_fusion.2), kind=kOutput, calls=%fused_computation.2 | convolution fusion | flops 4032430080 | bytes 10761216 | tf_op jit(solution)/shard_map/dot_general | solution.py:49
  173.2 7.3 %pad_maximum_fusion = bf16[768,5120]{1,0:T(8,128)(2,1)} fusion(bf16[768,2560]{1,0:T(8,128)(2,1)} %add_convert_fusion, bf16[768,2560]{1,0:T(8,128)(2,1)} %fusion.7), kind=kLoop, calls=%fused_computation | loop fusion | flops 15728640 | bytes 15728640 | tf_op jit(solution)/shard_map/concatenate | solution.py:56
  180.5 3.0 multiply_reduce_fusion
  183.5 12.7 %psum.7 = f32[1,2560]{1,0:T(1,128)S(1)} all-reduce(f32[1,2560]{1,0:T(1,128)S(1)} %all_gather.10), channel_id=1, replica_groups=mesh['expert'=32,'tensor'=4] {'tensor'}, use_global_device_ids=true, to_apply=%region_5.6 | all-reduce | flops 2560 | bytes 20480 | tf_op jit(solution)/shard_map/psum | solution.py:53
  196.3 29.3 %all-gather = f32[32,1,2560]{2,1,0:T(1,128)S(1)} all-gather(f32[1,1,2560]{2,1,0:T(1,128)S(1)} %bitcast.35), channel_id=1, replica_groups=mesh['expert'=32,'tensor'=4] {'expert'}, dimensions={0}, use_global_device_ids=true | all-gather | bytes 337920 | tf_op jit(solution)/shard_map/all_gather | solution.py:54
  225.6 0.7 copy.14
  226.3 32.3 %reduce-scatter.2.cloned.1.call-done = bf16[192,5120]{1,0:T(8,128)(2,1)} async-done(((bf16[768,5120]{1,0:T(8,128)(2,1)}), bf16[192,5120]{1,0:T(8,128)(2,1)}) %reduce-scatter.2.cloned.1.call-update) | async-done | bytes 1966096 | tf_op jit(solution)/shard_map/reduce_scatter | solution.py:55
  258.6 4.2 %reshape.52 = bf16[32,6,5120]{2,1,0:T(8,128)(2,1)} reshape(bf16[192,5120]{1,0:T(8,128)(2,1)} %reduce-scatter.2.cloned.1.call-done) | data formatting | bytes 3932160 | tf_op jit(solution)/shard_map/reshape | solution.py:59
  262.8 7.8 %all-to-all-start.1 = ((bf16[32,6,5120]{2,1,0:T(8,128)(2,1)}), bf16[32,6,5120]{2,1,0:T(8,128)(2,1)S(1)}, u32[]{:S(2)}, u32[]{:S(2)}) async-start(bf16[32,6,5120]{2,1,0:T(8,128)(2,1)} %reshape.52), calls=%async_computation.2 | async-start | bytes 5242880 | tf_op jit(solution)/shard_map/all_to_all | solution.py:58
  270.6 9.4 %fusion.10 = bf16[1,2560,1024]{2,1,0:T(8,128)(2,1)} fusion(bf16[768,1024]{1,0:T(8,128)(2,1)} %copy-done.4, bf16[768,5120]{1,0:T(8,128)(2,1)} %all-gather.3.cloned.1.call-done), kind=kOutput, calls=%fused_computation.14 | convolution fusion | flops 4029153280 | bytes 10747904 | tf_op jit(solution)/shard_map/dot_general | solution.py:46
  280.0 8.2 %fusion.11 = bf16[1,1024,2560]{2,1,0:T(8,128)(2,1)} fusion(bf16[768,5120]{1,0:T(8,128)(2,1)} %all-gather.3.cloned.1.call-done, f32[768,1024]{1,0:T(8,128)S(1)} %copy-done.3), kind=kOutput, calls=%fused_computation.15 | convolution fusion | flops 4033085440 | bytes 12320768 | tf_op jit(solution)/shard_map/dot_general | solution.py:45
  288.2 16.3 %all-to-all-done.1 = bf16[32,6,5120]{2,1,0:T(8,128)(2,1)S(1)} async-done(((bf16[32,6,5120]{2,1,0:T(8,128)(2,1)}), bf16[32,6,5120]{2,1,0:T(8,128)(2,1)S(1)}, u32[]{:S(2)}, u32[]{:S(2)}) %all-to-all-start.1) | async-done | bytes 1966112 | tf_op jit(solution)/shard_map/all_to_all | solution.py:58
  304.5 2.1 reshape.53
  306.6 2.1 fusion.23
  308.7 1.0 fusion.18
  309.7 0.9 slice.36
  (20 shorter events, 0.2 us)
Async XLA Ops:
  7.2 134.5 %all-gather.3.cloned.1.call-start = ((), (), s32[]{:S(2)}) async-start(), calls=%async_computation.3 | async-start | bytes 9830400 | tf_op jit(solution)/shard_map/all_gather | solution.py:32
  61.1 4.2 %copy-start.1 = (bf16[2560,32]{0,1:T(8,128)(2,1)S(1)}, bf16[2560,32]{0,1:T(8,128)(2,1)}, u32[]{:S(2)}) copy-start(bf16[2560,32]{0,1:T(8,128)(2,1)} %param.10) | copy-start | bytes 491524
  65.3 193.3 %reduce-scatter.2.cloned.1.call-start = ((), (), s32[]{:S(2)}) async-start(), calls=%async_computation.4 | async-start | bytes 9830400 | tf_op jit(solution)/shard_map/reduce_scatter | solution.py:55
  149.0 10.7 %copy-start.2 = (f32[768,1024]{1,0:T(8,128)}, f32[768,1024]{1,0:T(8,128)S(1)}, u32[]{:S(2)}) copy-start(f32[768,1024]{1,0:T(8,128)S(1)} %fusion.5) | copy-start | bytes 9437188
  149.0 9.5 %copy-start = (bf16[768,5120]{1,0:T(8,128)(2,1)S(1)}, bf16[768,5120]{1,0:T(8,128)(2,1)}, u32[]{:S(2)}) copy-start(bf16[768,5120]{1,0:T(8,128)(2,1)} %all-gather.3.cloned.1.call-done) | copy-start | bytes 23592964
  158.4 8.9 %slice-start = ((s8[5242880]{0:T(1024)(128)(4,1)}), s8[4194304]{0:T(1024)(128)(4,1)S(1)}, s32[]{:S(2)}) async-start(s8[5242880]{0:T(1024)(128)(4,1)} %bitcast.38), calls=%async_computation.5 | async-start | bytes 8388608
  159.7 7.6 %slice-start.1 = ((s8[5242880]{0:T(1024)(128)(4,1)}), s8[1048576]{0:T(1024)(128)(4,1)S(1)}, s32[]{:S(2)}) async-start(s8[5242880]{0:T(1024)(128)(4,1)} %bitcast.38), calls=%async_computation.6 | async-start | bytes 2097152
  167.3 5.9 %copy-start.4 = (bf16[768,1024]{1,0:T(8,128)(2,1)}, bf16[768,1024]{1,0:T(8,128)(2,1)S(1)}, u32[]{:S(2)}) copy-start(bf16[768,1024]{1,0:T(8,128)(2,1)S(1)} %get-tuple-element.6) | copy-start | bytes 4718596
  262.8 41.7 %all-to-all-start.1 = ((bf16[32,6,5120]{2,1,0:T(8,128)(2,1)}), bf16[32,6,5120]{2,1,0:T(8,128)(2,1)S(1)}, u32[]{:S(2)}, u32[]{:S(2)}) async-start(bf16[32,6,5120]{2,1,0:T(8,128)(2,1)} %reshape.52), calls=%async_computation.2 | async-start | bytes 5242880 | tf_op jit(solution)/shard_map/all_to_all | solution.py:58
  270.6 9.4 %copy-start.3 = (f32[768,1024]{1,0:T(8,128)S(1)}, f32[768,1024]{1,0:T(8,128)}, u32[]{:S(2)}) copy-start(f32[768,1024]{1,0:T(8,128)} %copy-done.2) | copy-start | bytes 9437188
Sparse Core Ops, SparseCore 0:
  65.4 76.1 all-gather.2
  180.7 77.9 reduce-scatter.1

commit v2 on v1

v2 whole, which is shorter than its diff:
```python
import jax
import jax.numpy as jnp
from jax import lax
from jax.experimental import pallas as pl
from jax.experimental.pallas import tpu as pltpu
from jax.sharding import PartitionSpec as P

F32, BF16, I32 = jnp.float32, jnp.bfloat16, jnp.int32
MESH = pl.DeviceIdType.MESH

NZ, NQ, NT = 4, 8, 4
EXPERTS = NZ * NQ
ROWS, MOST = 128, 6
SLOTS = EXPERTS * MOST
BOTH = 2 * SLOTS
C, NC = 512, 5
H = 1024
N = 256


def dot(a, b, dims=((1,), (0,))):
    return lax.dot_general(a, b, (dims, ((), ())), preferred_element_type=F32)


NTD = ((1,), (1,))
TND = ((0,), (0,))


def iota(shape, axis):
    return lax.broadcasted_iota(I32, shape, axis).astype(F32)


def onehot(mask):
    return jnp.where(mask, 1.0, 0.0).astype(BF16)


def div(a, b):
    return jnp.floor((a + 0.5) * (1.0 / b))


def source_1(o):
    q = div(o, 2 * NZ * MOST)
    r = o - q * (2 * NZ * MOST)
    a = div(r, NZ * MOST)
    r = r - a * (NZ * MOST)
    z = div(r, MOST)
    k = r - z * MOST
    return z * (NQ * 2 * MOST) + q * (2 * MOST) + a * MOST + k


def source_2(o):
    a = div(o, SLOTS)
    r = o - a * SLOTS
    q = div(r, NZ * MOST)
    m = r - q * (NZ * MOST)
    return q * (2 * NZ * MOST) + a * (NZ * MOST) + m


def kernel(
    ids_ref, live_ref, router_ref, tok_ref, og_ref, up_hbm, down_hbm,
    mixed_ref, tgrad_ref, upg_hbm, downg_hbm, rgrad_ref,
    box, inz, outx, inx, yb, wu, wd, hid, dh, act, hc, lg, gate_s, slope_s, slope3,
    sa, ra, sb, rb, rx, rz, gsu, gsd, p1, p1t, p2, p2t, plc, pltx, pltc, rrow,
    vy, vx, vz,
    wsem, zs, zr, xs, xr, ys, yr, as_, ar, bs, br, xs2, xr2, zs2, zr2, gsem,
    vys, vyr, vxs, vxr, vzs, vzr,
):
    me = lax.axis_index("expert")
    t = lax.axis_index("tensor")
    z, q = me // NQ, me % NQ

    def zpeer(d):
        return (((z + d) % NZ) * NQ + q, t)

    def xpeer(d):
        return (z * NQ + (q + d) % NQ, t)

    def ypeer(d):
        return (me, (t + d) % NT)

    def remote(src, dst, ssem, rsem, peer):
        return pltpu.make_async_remote_copy(
            src_ref=src, dst_ref=dst, send_sem=ssem, recv_sem=rsem,
            device_id=peer, device_id_type=MESH,
        )

    def weights(s):
        cols = pl.ds(pl.multiple_of(s * C, C), C)
        return (
            pltpu.make_async_copy(up_hbm.at[0, cols, :], wu.at[s], wsem.at[0, s]),
            pltpu.make_async_copy(down_hbm.at[0, :, cols], wd.at[s], wsem.at[1, s]),
        )

    def zcopy(s, d):
        return remote(box.at[s, (z + d) % NZ], inz.at[s, z], zs.at[s, d], zr.at[s, d], zpeer(d))

    def zland(s, d):
        return remote(box.at[s, z], inz.at[s, (z + NZ - d) % NZ], zs.at[s, d], zr.at[s, d], zpeer(d))

    def xcopy(s, d):
        return remote(outx.at[s, (q + d) % NQ], inx.at[s, q], xs.at[s, d], xr.at[s, d], xpeer(d))

    def xland(s, d):
        return remote(outx.at[s, q], inx.at[s, (q + NQ - d) % NQ], xs.at[s, d], xr.at[s, d], xpeer(d))

    left, right = (t + NT - 1) % NT, (t + 1) % NT
    far = (t + 2) % NT
    lo, hi = pl.ds(0, SLOTS), pl.ds(SLOTS, SLOTS)

    def ycopy(s, i):
        if i == 0:
            src, peer = yb.at[s, t], ypeer(1)
        elif i == 1:
            src, peer = yb.at[s, t], ypeer(NT - 1)
        elif i == 2:
            src, peer = yb.at[s, left, lo], ypeer(1)
        else:
            src, peer = yb.at[s, right, hi], ypeer(NT - 1)
        return remote(src, src, ys.at[s, i], yr.at[s, i], peer)

    def yland(s, i):
        dst = (yb.at[s, left], yb.at[s, right], yb.at[s, far, lo], yb.at[s, far, hi])[i]
        return remote(dst, dst, ys.at[s, i], yr.at[s, i], ypeer(1))

    def acopy(s, i):
        return remote(sa.at[s, i], ra.at[s, i], as_.at[s, i], ar.at[s, i], ypeer((1, NT - 1)[i]))

    def bcopy(s, i):
        return remote(sb.at[s, i], rb.at[s, i], bs.at[s, i], br.at[s, i], ypeer((1, NT - 1)[i]))

    def x2copy(s, d):
        return remote(outx.at[s, (q + d) % NQ], rx.at[s, q], xs2.at[s, d], xr2.at[s, d], xpeer(d))

    def x2land(s, d):
        return remote(outx.at[s, q], rx.at[s, (q + NQ - d) % NQ], xs2.at[s, d], xr2.at[s, d], xpeer(d))

    def z2copy(s, d):
        return remote(box.at[s, (z + d) % NZ], rz.at[s, z], zs2.at[s, d], zr2.at[s, d], zpeer(d))

    def z2land(s, d):
        return remote(box.at[s, z], rz.at[s, (z + NZ - d) % NZ], zs2.at[s, d], zr2.at[s, d], zpeer(d))

    def vycopy(d):
        return remote(vy.at[t], vy.at[t], vys.at[d], vyr.at[d], ypeer(d))

    def vyland(d):
        dst = vy.at[(t + NT - d) % NT]
        return remote(dst, dst, vys.at[d], vyr.at[d], ypeer(d))

    def vxcopy(d):
        return remote(vx.at[q], vx.at[q], vxs.at[d], vxr.at[d], xpeer(d))

    def vxland(d):
        dst = vx.at[(q + NQ - d) % NQ]
        return remote(dst, dst, vxs.at[d], vxr.at[d], xpeer(d))

    def vzcopy(d):
        return remote(vx, vz.at[z], vzs.at[d], vzr.at[d], zpeer(d))

    def vzland(d):
        return remote(vx, vz.at[(z + NZ - d) % NZ], vzs.at[d], vzr.at[d], zpeer(d))

    for s in range(NC):
        for copy in weights(s):
            copy.start()

    barrier = pltpu.get_barrier_semaphore()
    for d in range(1, NZ):
        pl.semaphore_signal(barrier, inc=1, device_id=zpeer(d), device_id_type=MESH)
    for d in range(1, NQ):
        pl.semaphore_signal(barrier, inc=1, device_id=xpeer(d), device_id_type=MESH)
    for d in range(1, NT):
        pl.semaphore_signal(barrier, inc=1, device_id=ypeer(d), device_id_type=MESH)

    ids = ids_ref[...].astype(F32)
    chosen = ids == iota((ROWS, EXPERTS), 1)
    tri = onehot(iota((ROWS, ROWS), 0) > iota((ROWS, ROWS), 1))
    counts = dot(tri, onehot(chosen))
    rank = jnp.sum(jnp.where(chosen, counts, 0.0), axis=1, keepdims=True)
    logits = dot(tok_ref[...], router_ref[...])
    gate = jax.nn.sigmoid(jnp.sum(jnp.where(chosen, logits, 0.0), axis=1, keepdims=True))
    gate_s[...] = jnp.broadcast_to(gate, (ROWS, 128))
    live = lax.broadcasted_iota(I32, (ROWS, 1), 0) < live_ref[0]
    target = jnp.where(live, ids * (2.0 * MOST) + rank, -1000.0)
    diag = iota((ROWS, ROWS), 0) == iota((ROWS, ROWS), 1)
    target_row = jnp.sum(jnp.where(diag, target, 0.0), axis=0, keepdims=True)
    slot = iota((BOTH, ROWS), 0)
    plc[:, :ROWS] = onehot(slot == target_row)
    plc[:, ROWS:] = onehot(slot == target_row + MOST)
    lane = iota((ROWS, BOTH), 1)
    pltx[...] = onehot(lane == target)
    pltc[...] = onehot(lane == target + MOST)
    column, line = iota((BOTH, 1), 0), iota((1, BOTH), 1)
    across, down = iota((BOTH, BOTH), 1), iota((BOTH, BOTH), 0)
    p1[...] = onehot(source_1(column) == across)
    p1t[...] = onehot(source_1(line) == down)
    p2[...] = onehot(source_2(column) == across)
    p2t[...] = onehot(source_2(line) == down)

    pl.semaphore_wait(barrier, NZ + NQ + NT - 3)

    def piece(s):
        return pl.ds(pl.multiple_of(s * C, C), C)

    @pl.loop(0, NC)
    def _(s):
        cot = (gate_s[:, :1] * og_ref[:, piece(s)].astype(F32)).astype(BF16)
        both = jnp.concatenate([tok_ref[:, piece(s)], cot], axis=0)
        box[s] = dot(plc[...], both).astype(BF16).reshape(NZ, NQ * 2 * MOST, C)
        for d in range(1, NZ):
            zcopy(s, d).start()
        inz[s, z] = box[s, z]

    hid[...] = jnp.zeros_like(hid)
    dh[...] = jnp.zeros_like(dh)
    lg[...] = jnp.zeros_like(lg)
    own = onehot(iota((8, EXPERTS), 1) == me.astype(F32))

    @pl.loop(0, NC)
    def _(s):
        rrow[s] = dot(own, router_ref[piece(s), :], NTD)

    def rows_of(s):
        return yb[s, :, :SLOTS, :].reshape(NT * SLOTS, C)

    def cots_of(s):
        return yb[s, :, SLOTS:, :].reshape(NT * SLOTS, C)

    def dispatch_1(s):
        for d in range(1, NZ):
            zland(s, d).wait_recv()
        outx[s] = dot(p1[...], inz[s].reshape(BOTH, C)).astype(BF16).reshape(NQ, 2 * NZ * MOST, C)
        for d in range(1, NQ):
            xcopy(s, d).start()
        inx[s, q] = outx[s, q]

    def dispatch_2(s):
        for d in range(1, NQ):
            xland(s, d).wait_recv()
        yb[s, t] = dot(p2[...], inx[s].reshape(BOTH, C)).astype(BF16)
        ycopy(s, 0).start()
        ycopy(s, 1).start()

    def dispatch_3(s):
        yland(s, 0).wait_recv()
        ycopy(s, 2).start()
        yland(s, 1).wait_recv()
        ycopy(s, 3).start()

    def dispatch_4(s):
        yland(s, 2).wait_recv()
        yland(s, 3).wait_recv()
        for copy in weights(s):
            copy.wait()
        lg[...] += dot(rows_of(s), router_ref[piece(s), :])

        @pl.loop(0, H // N)
        def _(n):
            part = pl.ds(pl.multiple_of(n * N, N), N)
            hid[:, part] += dot(rows_of(s), wu[s, :, part])
            dh[:, part] += dot(cots_of(s), wd[s, part, :], NTD)

    @pl.loop(0, NC + 4)
    def _(i):
        @pl.when(i < NC)
        def _():
            dispatch_1(i)

        @pl.when((i >= 1) & (i < NC + 1))
        def _():
            dispatch_2(i - 1)

        @pl.when((i >= 3) & (i < NC + 3))
        def _():
            dispatch_3(i - 3)

        @pl.when(i >= 4)
        def _():
            dispatch_4(i - 4)

    @pl.loop(0, NC)
    def _(s):
        for d in range(1, NZ):
            zcopy(s, d).wait_send()
        for d in range(1, NQ):
            xcopy(s, d).wait_send()
        for i in range(4):
            ycopy(s, i).wait_send()

    BR = 32

    @pl.loop(0, NT * SLOTS // BR)
    def _(b):
        r = pl.ds(pl.multiple_of(b * BR, BR), BR)
        v, back = hid[r, :], dh[r, :]
        sig = 1.0 / (1.0 + jnp.exp(-v))
        a = (v * sig).astype(BF16)
        act[r, :] = a
        hc[r, :] = (back * (sig * (1.0 + v * (1.0 - sig)))).astype(BF16)
        part = jnp.sum(a.astype(F32) * back, axis=1, keepdims=True)
        mine = iota((BR, EXPERTS), 1) == me.astype(F32)
        logit = jnp.sum(jnp.where(mine, lg[r, :], 0.0), axis=1, keepdims=True)
        slope = part * (1.0 - 1.0 / (1.0 + jnp.exp(-logit)))
        slope_s[r, :] = jnp.broadcast_to(slope, (BR, 128))
        s1 = slope.astype(BF16).astype(F32)
        s2 = (slope - s1).astype(BF16).astype(F32)
        s3 = slope - s1 - s2
        k = iota((BR, 128), 1)
        slope3[r, :] = jnp.where(
            k == 0.0, s1, jnp.where(k == 1.0, s2, jnp.where(k == 2.0, s3, 0.0))
        ).astype(BF16)

    def partial(s, b):
        r = pl.ds(pl.multiple_of(b * SLOTS, SLOTS), SLOTS)
        value = dot(act[r, :], wd[s])
        grad = dot(hc[r, :], wu[s], NTD) + slope_s[r, :1] * rrow[s, :1, :]
        return value, grad

    def return_0(s):
        value, grad = partial(s, far)
        sa[s, 0] = value.astype(BF16)
        sa[s, 1] = grad.astype(BF16)
        acopy(s, 0).start()
        acopy(s, 1).start()

    def return_1(s):
        value, grad = partial(s, right)
        acopy(s, 0).wait_recv()
        sb[s, 0, lo] = (value + ra[s, 0].astype(F32)).astype(BF16)
        sb[s, 0, hi] = grad.astype(BF16)
        bcopy(s, 0).start()
        value, grad = partial(s, left)
        acopy(s, 1).wait_recv()
        sb[s, 1, lo] = value.astype(BF16)
        sb[s, 1, hi] = (grad + ra[s, 1].astype(F32)).astype(BF16)
        bcopy(s, 1).start()

    def return_2(s):
        value, grad = partial(s, t)
        bcopy(s, 0).wait_recv()
        bcopy(s, 1).wait_recv()
        value = value + rb[s, 0, :SLOTS, :].astype(F32) + rb[s, 1, :SLOTS, :].astype(F32)
        grad = grad + rb[s, 0, SLOTS:, :].astype(F32) + rb[s, 1, SLOTS:, :].astype(F32)
        both = jnp.concatenate([value, grad], axis=0).astype(BF16)
        outx[s] = dot(p2t[...], both).astype(BF16).reshape(NQ, 2 * NZ * MOST, C)
        for d in range(1, NQ):
            x2copy(s, d).start()
        rx[s, q] = outx[s, q]

    def return_3(s):
        for d in range(1, NQ):
            x2land(s, d).wait_recv()
        box[s] = dot(p1t[...], rx[s].reshape(BOTH, C)).astype(BF16).reshape(NZ, NQ * 2 * MOST, C)
        for d in range(1, NZ):
            z2copy(s, d).start()
        rz[s, z] = box[s, z]

    def return_4(s):
        for d in range(1, NZ):
            z2land(s, d).wait_recv()
        got = rz[s].reshape(BOTH, C)
        mixed_ref[:, piece(s)] = (gate_s[:, :1] * dot(pltx[...], got)).astype(BF16)
        tgrad_ref[:, piece(s)] = dot(pltc[...], got).astype(BF16)

    def grads_out(s):
        return (
            pltpu.make_async_copy(gsu.at[s % 2], upg_hbm.at[0, piece(s), :], gsem.at[0, s]),
            pltpu.make_async_copy(gsd.at[s % 2], downg_hbm.at[0, :, piece(s)], gsem.at[1, s]),
        )

    def grads(s):
        @pl.when(s >= 2)
        def _():
            for copy in grads_out(s - 2):
                copy.wait()

        @pl.loop(0, H // N)
        def _(n):
            part = pl.ds(pl.multiple_of(n * N, N), N)
            gsd[s % 2, part, :] = dot(act[:, part], cots_of(s), TND).astype(BF16)
            gsu[s % 2, :, part] = dot(rows_of(s), hc[:, part], TND).astype(BF16)

        for copy in grads_out(s):
            copy.start()

    def vector_0():
        @pl.loop(0, NC)
        def _(s):
            three = dot(slope3[...], rows_of(s), TND)
            vy[t, :, piece(s)] = jnp.sum(three, axis=0, keepdims=True)

        for d in range(1, NT):
            vycopy(d).start()

    def vector_1():
        for d in range(1, NT):
            vyland(d).wait_recv()
        vx[q] = (vy[0] + vy[1]) + (vy[2] + vy[3])
        for d in range(1, NQ):
            vxcopy(d).start()

    def vector_2():
        for d in range(1, NQ):
            vxland(d).wait_recv()
        for d in range(1, NZ):
            vzcopy(d).start()
        vz[z] = vx[...]

    @pl.loop(0, NC + 4)
    def _(j):
        @pl.when(j < NC)
        def _():
            return_0(j)

        @pl.when((j >= 1) & (j < NC + 1))
        def _():
            return_1(j - 1)

        @pl.when(j == 1)
        def _():
            vector_0()

        @pl.when(j == 3)
        def _():
            vector_1()

        @pl.when(j == 5)
        def _():
            vector_2()

        @pl.when((j >= 1) & (j < NC + 1))
        def _():
            grads(j - 1)

        @pl.when((j >= 2) & (j < NC + 2))
        def _():
            return_2(j - 2)

        @pl.when((j >= 3) & (j < NC + 3))
        def _():
            return_3(j - 3)

        @pl.when(j >= 4)
        def _():
            return_4(j - 4)

    for d in range(1, NZ):
        vzland(d).wait_recv()
    rgrad_ref[...] = vz[...].reshape(EXPERTS, 1, C * NC)
    for d in range(1, NT):
        vycopy(d).wait_send()
    for d in range(1, NQ):
        vxcopy(d).wait_send()
    for d in range(1, NZ):
        vzcopy(d).wait_send()

    @pl.loop(0, NC)
    def _(s):
        for i in range(2):
            acopy(s, i).wait_send()
            bcopy(s, i).wait_send()
        for d in range(1, NQ):
            x2copy(s, d).wait_send()
        for d in range(1, NZ):
            z2copy(s, d).wait_send()

    for s in (NC - 2, NC - 1):
        for copy in grads_out(s):
            copy.wait()


def per_device(tokens, expert_ids, live_counts, router, up_weight, down_weight, out_grad):
    width = tokens.shape[1]
    assert tokens.shape == (ROWS, C * NC) and router.shape[1] == EXPERTS
    assert up_weight.shape == (1, C * NC, H)
    vmem = pl.BlockSpec(memory_space=pltpu.VMEM)
    smem = pl.BlockSpec(memory_space=pltpu.SMEM)
    hbm = pl.BlockSpec(memory_space=pl.ANY)
    all_rows = NT * SLOTS
    V, DMA = pltpu.VMEM, pltpu.SemaphoreType.DMA
    scratch = [
        V((NC, NZ, NQ * 2 * MOST, C), BF16),
        V((NC, NZ, NQ * 2 * MOST, C), BF16),
        V((NC, NQ, 2 * NZ * MOST, C), BF16),
        V((NC, NQ, 2 * NZ * MOST, C), BF16),
        V((NC, NT, BOTH, C), BF16),
        V((NC, C, H), BF16),
        V((NC, H, C), BF16),
        V((all_rows, H), F32),
        V((all_rows, H), F32),
        V((all_rows, H), BF16),
        V((all_rows, H), BF16),
        V((all_rows, EXPERTS), F32),
        V((ROWS, 128), F32),
        V((all_rows, 128), F32),
        V((all_rows, 128), BF16),
        V((NC, 2, SLOTS, C), BF16),
        V((NC, 2, SLOTS, C), BF16),
        V((NC, 2, BOTH, C), BF16),
        V((NC, 2, BOTH, C), BF16),
        V((NC, NQ, 2 * NZ * MOST, C), BF16),
        V((NC, NZ, NQ * 2 * MOST, C), BF16),
        V((2, C, H), BF16),
        V((2, H, C), BF16),
        V((BOTH, BOTH), BF16),
        V((BOTH, BOTH), BF16),
        V((BOTH, BOTH), BF16),
        V((BOTH, BOTH), BF16),
        V((BOTH, 2 * ROWS), BF16),
        V((ROWS, BOTH), BF16),
        V((ROWS, BOTH), BF16),
        V((NC, 8, C), F32),
        V((NT, 1, width), F32),
        V((NQ, 1, width), F32),
        V((NZ, NQ, 1, width), F32),
        DMA((2, NC)),
        DMA((NC, NZ)), DMA((NC, NZ)), DMA((NC, NQ)), DMA((NC, NQ)), DMA((NC, 4)), DMA((NC, 4)),
        DMA((NC, 2)), DMA((NC, 2)), DMA((NC, 2)), DMA((NC, 2)),
        DMA((NC, NQ)), DMA((NC, NQ)), DMA((NC, NZ)), DMA((NC, NZ)),
        DMA((2, NC)),
        DMA((NT,)), DMA((NT,)), DMA((NQ,)), DMA((NQ,)), DMA((NZ,)), DMA((NZ,)),
    ]
    S = jax.ShapeDtypeStruct
    mixed, tgrad, upg, downg, rgrad = pl.pallas_call(
        kernel,
        out_shape=(
            S((ROWS, width), BF16),
            S((ROWS, width), BF16),
            S((1, width, H), BF16),
            S((1, H, width), BF16),
            S((EXPERTS, 1, width), F32),
        ),
        in_specs=[vmem, smem, vmem, vmem, vmem, hbm, hbm],
        out_specs=(vmem, vmem, hbm, hbm, vmem),
        scratch_shapes=scratch,
        compiler_params=pltpu.CompilerParams(
            collective_id=0, has_side_effects=True, vmem_limit_bytes=67043328
        ),
    )(expert_ids, live_counts, router, tokens, out_grad, up_weight, down_weight)
    return (mixed, tgrad, upg, downg, rgrad.reshape(EXPERTS, width).T)


def solution(mesh):
    rows = P(("expert", "tensor"), None)
    in_specs = (
        rows,
        rows,
        P(("expert", "tensor")),
        P(),
        P("expert", None, "tensor"),
        P("expert", "tensor", None),
        rows,
    )
    out_specs = (rows, rows, P("expert", None, "tensor"), P("expert", "tensor", None), P())
    return jax.shard_map(
        per_device, mesh=mesh, in_specs=in_specs, out_specs=out_specs, check_vma=False
    )
```

time: 319 us -> 202 us (0.63)
  Pallas kernels: 0 us -> 183 us
  waiting for transfers between devices: 125 us -> 0 us
  blocking collectives: 85.3 us -> 0 us
  matrix products: 55.6 us -> 0 us
  other arithmetic: 14.2 us -> 0.01 us
  between operations: 14.9 us -> 1.29 us
  starting transfers between devices: 7.84 us -> 0 us
    pallas_call x0 -> x1, Pallas kernels: none -> 183 us  [per_device(): pl.pallas_call(kernel, out_shape=(S((ROWS, width), BF16), S((ROWS, width)...]
    all_gather x1 -> x0, waiting for transfers between devices: 76.2 us -> none  [per_device(): rows_all = lax.all_gather(inbox, 'tensor', axis=0, tiled=True)]
    dot_general x10 -> x0, matrix products: 55.6 us -> none  [the longest x1 9.45 us: per_device(): value = jnp.dot(active, w_down, preferred_element_type=F32).astype(BF16)]
    all_to_all x1 -> x0, blocking collectives: 43.2 us -> none  [per_device(): lax.all_to_all(box.reshape(experts, most, 2 * width), 'expert', split_axi...]
    reduce_scatter x1 -> x0, waiting for transfers between devices: 32.3 us -> none  [per_device(): lax.psum_scatter(jnp.concatenate([value, grad], axis=1), 'tensor', scatte...]
    all_gather x1 -> x0, blocking collectives: 29.3 us -> none  [per_device(): router_grad = lax.all_gather(router_col, 'expert', axis=0).T]
    all_to_all x1 -> x0, waiting for transfers between devices: 16.3 us -> none  [per_device(): lax.all_to_all(summed.reshape(experts, most, 2 * width), 'expert', split_...]
    unnamed x15 -> x11, local copies, waits for them, and re-layouts: 0.79 us -> 17.1 us
  transfers between devices with their start and end apart: 3 -> 0, of which waited for: 3 -> 0; matrix products, arithmetic and copies ran while one was open for 7% -> 0% of each run, Pallas kernels for 0% -> 0%
where the time goes in v2:
time: 202 us
  Pallas kernels  183 us (91%)
  local copies, waits for them, and re-layouts  17.1 us (8%)
    pallas_call x1, Pallas kernels, per_device(): pl.pallas_call(kernel, out_shape=(S((ROWS, width), BF16), S((ROWS, width)...  183 us
    unnamed x11, local copies, waits for them, and re-layouts  17.1 us

profile of v2, /device:TPU:1, one launch (start us, length us, event | category | flops | bytes accessed | tf_op | source)
XLA Modules:
  0.0 201.8 jit_solution(6572746095990090923)
XLA Ops:
  1.3 1.4 copy.12.ids_ref
  2.7 2.0 copy.13.router_ref
  4.7 183.5 %shard_map.110 = (bf16[128,2560]{1,0:T(8,128)(2,1)}, bf16[128,2560]{1,0:T(8,128)(2,1)}, bf16[1,2560,1024]{2,1,0:T(8,128)(2,1)}, bf16[1,1024,2560]{2,1,0:T(8,128)(2,1)}, f32[32,1,2560]{2,1,0:T(1,128)}) custom-call(s32[128,1]{1,0:T(8,128)} %copy.12.ids_ref, s32[1]{0:T(128)S(6)} %copy.21.live_ref, bf16[2560,32]{1,0:T(8,128)(2,1)} %copy.13.router_ref, ...), custom_call_target="tpu_custom_call" | custom-call | tf_op jit(solution)/shard_map/pallas_call | solution.py:524
  188.1 1.7 copy.16
  189.8 2.0 copy.22
  191.8 0.0 slice-start
  191.8 2.1 %copy.23 = bf16[128,2560]{1,0:T(8,128)(2,1)} copy(bf16[128,2560]{1,0:T(8,128)(2,1)} %get-tuple-element.21) | data formatting | bytes 1310720
  193.9 0.0 slice-start.1
  193.9 5.5 %copy.24 = bf16[1,2560,1024]{2,1,0:T(8,128)(2,1)} copy(bf16[1,2560,1024]{2,1,0:T(8,128)(2,1)} %get-tuple-element.22) | data formatting | bytes 10485760
  199.4 0.0 slice-done
  199.4 0.0 slice-done.1
  199.4 2.4 %copy.25 = bf16[1,1024,2560]{2,1,0:T(8,128)(2,1)} copy(bf16[1,1024,2560]{2,1,0:T(8,128)(2,1)S(1)} %bitcast.6) | data formatting | bytes 10485760
  (1 shorter events, 0.0 us)
Async XLA Ops:
  191.8 7.6 %slice-start = ((s8[5242880]{0:T(1024)(128)(4,1)}), s8[4194304]{0:T(1024)(128)(4,1)S(1)}, s32[]{:S(2)}) async-start(s8[5242880]{0:T(1024)(128)(4,1)} %bitcast.5), calls=%async_computation | async-start | bytes 8388608
  193.9 5.5 %slice-start.1 = ((s8[5242880]{0:T(1024)(128)(4,1)}), s8[1048576]{0:T(1024)(128)(4,1)S(1)}, s32[]{:S(2)}) async-start(s8[5242880]{0:T(1024)(128)(4,1)} %bitcast.5), calls=%async_computation.1 | async-start | bytes 2097152

commit v3 on v2

v3 whole, which is shorter than its diff:
```python
import jax
import jax.numpy as jnp
from jax import lax
from jax.experimental import pallas as pl
from jax.experimental.pallas import tpu as pltpu
from jax.sharding import PartitionSpec as P

F32, BF16, I32 = jnp.float32, jnp.bfloat16, jnp.int32
MESH = pl.DeviceIdType.MESH

NZ, NQ, NT = 4, 8, 4
EXPERTS = NZ * NQ
ROWS, MOST = 128, 6
SLOTS = EXPERTS * MOST
BOTH = 2 * SLOTS
C, NC = 512, 5
NN, NS = 3, 2
NU = 2 * NS
ZR, XR = NQ * 2 * MOST, 2 * NZ * MOST
H = 1024
N = 256


def dot(a, b, dims=((1,), (0,))):
    return lax.dot_general(a, b, (dims, ((), ())), preferred_element_type=F32)


NTD = ((1,), (1,))
TND = ((0,), (0,))


def iota(shape, axis):
    return lax.broadcasted_iota(I32, shape, axis).astype(F32)


def onehot(mask):
    return jnp.where(mask, 1.0, 0.0).astype(BF16)


def div(a, b):
    return jnp.floor((a + 0.5) * (1.0 / b))


def source_1(o):
    q = div(o, 2 * NZ * MOST)
    r = o - q * (2 * NZ * MOST)
    a = div(r, NZ * MOST)
    r = r - a * (NZ * MOST)
    z = div(r, MOST)
    k = r - z * MOST
    return z * (NQ * 2 * MOST) + q * (2 * MOST) + a * MOST + k


def source_2(o):
    a = div(o, SLOTS)
    r = o - a * SLOTS
    q = div(r, NZ * MOST)
    m = r - q * (NZ * MOST)
    return q * (2 * NZ * MOST) + a * (NZ * MOST) + m


def kernel(
    ids_ref, live_ref, router_ref, tok_ref, og_ref, up_hbm, down_hbm,
    mixed_ref, tgrad_ref, upg_hbm, downg_hbm, rgrad_ref,
    box, inz, outx, inx, ubox, uinz, uoutx, uinx, raw, yb, wu, wd, hid, dh, act, hc,
    lg, gate_s, slope_s, slope3, sa, ra, sb, rb, ua, ub, gsu, gsd,
    p1, p1t, p2, p2t, plc, pltx, pltc, rrow, vt, vy, vx, vz,
    wsem, zs, zr, xs, xr, ys, yr, as_, ar, bs, br, uzs, uzr, uxs, uxr, rs, rr,
    uas, uar, ubs, ubr, gsem, vts, vtr, vys, vyr, vxs, vxr, vzs, vzr, free,
):
    me = lax.axis_index("expert")
    t = lax.axis_index("tensor")
    z, q = me // NQ, me % NQ
    left, right, far = (t + NT - 1) % NT, (t + 1) % NT, (t + 2) % NT
    lo, hi = pl.ds(0, SLOTS), pl.ds(SLOTS, SLOTS)
    rlo, rhi = pl.ds(0, ROWS), pl.ds(ROWS, ROWS)
    ZD, XD, YD = range(1, NZ), range(1, NQ), range(1, NT)

    def zpeer(d):
        return (((z + d) % NZ) * NQ + q, t)

    def xpeer(d):
        return (z * NQ + (q + d) % NQ, t)

    def ypeer(d):
        return (me, (t + d) % NT)

    def remote(src, dst, ssem, rsem, peer):
        return pltpu.make_async_remote_copy(
            src_ref=src, dst_ref=dst, send_sem=ssem, recv_sem=rsem,
            device_id=peer, device_id_type=MESH,
        )

    def piece(s):
        return pl.ds(pl.multiple_of(s * C, C), C)

    def normal(n):
        return n + (n + 1) // 2

    def special(v):
        return 1 + 3 * v

    def weights(s):
        return (
            pltpu.make_async_copy(up_hbm.at[0, piece(s), :], wu.at[s], wsem.at[0, s]),
            pltpu.make_async_copy(down_hbm.at[0, :, piece(s)], wd.at[s], wsem.at[1, s]),
        )

    def zcopy(n, d):
        return remote(box.at[n, (z + d) % NZ], inz.at[n, z], zs.at[n, d], zr.at[n, d], zpeer(d))

    def zland(n, d):
        return remote(box.at[n, z], inz.at[n, (z + NZ - d) % NZ], zs.at[n, d], zr.at[n, d], zpeer(d))

    def xcopy(n, d):
        return remote(outx.at[n, (q + d) % NQ], inx.at[n, q], xs.at[n, d], xr.at[n, d], xpeer(d))

    def xland(n, d):
        return remote(outx.at[n, q], inx.at[n, (q + NQ - d) % NQ], xs.at[n, d], xr.at[n, d], xpeer(d))

    def uzcopy(u, d):
        return remote(ubox.at[u, (z + d) % NZ], uinz.at[u, z], uzs.at[u, d], uzr.at[u, d], zpeer(d))

    def uzland(u, d):
        return remote(ubox.at[u, z], uinz.at[u, (z + NZ - d) % NZ], uzs.at[u, d], uzr.at[u, d], zpeer(d))

    def uxcopy(u, d):
        return remote(uoutx.at[u, (q + d) % NQ], uinx.at[u, q], uxs.at[u, d], uxr.at[u, d], xpeer(d))

    def uxland(u, d):
        return remote(uoutx.at[u, q], uinx.at[u, (q + NQ - d) % NQ], uxs.at[u, d], uxr.at[u, d], xpeer(d))

    SIDE = (1, NT - 1, 1, NT - 1)

    def ycopy(n, i):
        s = normal(n)
        src = (yb.at[s, t], yb.at[s, t], yb.at[s, left, lo], yb.at[s, right, hi])[i]
        return remote(src, src, ys.at[n, i], yr.at[n, i], ypeer(SIDE[i]))

    def yland(n, i):
        s = normal(n)
        dst = (yb.at[s, left], yb.at[s, right], yb.at[s, far, lo], yb.at[s, far, hi])[i]
        return remote(dst, dst, ys.at[n, i], yr.at[n, i], ypeer(SIDE[i]))

    def rcopy(v, i):
        src = (raw.at[v, t], raw.at[v, t], raw.at[v, left, rlo], raw.at[v, right, rhi])[i]
        return remote(src, src, rs.at[v, i], rr.at[v, i], ypeer(SIDE[i]))

    def rland(v, i):
        dst = (raw.at[v, left], raw.at[v, right], raw.at[v, far, rlo], raw.at[v, far, rhi])[i]
        return remote(dst, dst, rs.at[v, i], rr.at[v, i], ypeer(SIDE[i]))

    def acopy(n, i):
        return remote(sa.at[n, i], ra.at[n, i], as_.at[n, i], ar.at[n, i], ypeer(SIDE[i]))

    def bcopy(n, i):
        return remote(sb.at[n, i], rb.at[n, i], bs.at[n, i], br.at[n, i], ypeer(SIDE[i]))

    def uacopy(v, i):
        src = raw.at[v, 2, (rlo, rhi)[i]]
        return remote(src, ua.at[v, i], uas.at[v, i], uar.at[v, i], ypeer(SIDE[i]))

    def ubcopy(v, i):
        return remote(raw.at[v, SIDE[i]], ub.at[v, i], ubs.at[v, i], ubr.at[v, i], ypeer(SIDE[i]))

    def vtcopy(d):
        return remote(vt.at[t], vt.at[t], vts.at[d], vtr.at[d], ypeer(d))

    def vtland(d):
        dst = vt.at[(t + NT - d) % NT]
        return remote(dst, dst, vts.at[d], vtr.at[d], ypeer(d))

    def vycopy(d):
        return remote(vy.at[t], vy.at[t], vys.at[d], vyr.at[d], ypeer(d))

    def vyland(d):
        dst = vy.at[(t + NT - d) % NT]
        return remote(dst, dst, vys.at[d], vyr.at[d], ypeer(d))

    def vxcopy(d):
        return remote(vx.at[q], vx.at[q], vxs.at[d], vxr.at[d], xpeer(d))

    def vxland(d):
        dst = vx.at[(q + NQ - d) % NQ]
        return remote(dst, dst, vxs.at[d], vxr.at[d], xpeer(d))

    def vzcopy(d):
        return remote(vx, vz.at[z], vzs.at[d], vzr.at[d], zpeer(d))

    def vzland(d):
        return remote(vx, vz.at[(z + NZ - d) % NZ], vzs.at[d], vzr.at[d], zpeer(d))

    for s in range(NC):
        for copy in weights(s):
            copy.start()

    barrier = pltpu.get_barrier_semaphore()
    for peers, ds in ((zpeer, ZD), (xpeer, XD), (ypeer, YD)):
        for d in ds:
            pl.semaphore_signal(barrier, inc=1, device_id=peers(d), device_id_type=MESH)

    diag = iota((ROWS, ROWS), 0) == iota((ROWS, ROWS), 1)

    def turned(line):
        return jnp.sum(jnp.where(diag, line, 0.0), axis=1, keepdims=True)

    ids = turned(ids_ref[...].astype(F32))
    chosen = ids == iota((ROWS, EXPERTS), 1)
    tri = onehot(iota((ROWS, ROWS), 0) > iota((ROWS, ROWS), 1))
    counts = dot(tri, onehot(chosen))
    rank = jnp.sum(jnp.where(chosen, counts, 0.0), axis=1, keepdims=True)
    logits = dot(tok_ref[...], router_ref[...], NTD)
    gate = jax.nn.sigmoid(jnp.sum(jnp.where(chosen, logits, 0.0), axis=1, keepdims=True))
    gate_s[...] = jnp.broadcast_to(gate, (ROWS, 128))
    live = lax.broadcasted_iota(I32, (ROWS, 1), 0) < live_ref[0]
    target = jnp.where(live, ids * (2.0 * MOST) + rank, -1000.0)
    vt[t] = jnp.sum(jnp.where(diag, target, 0.0), axis=0, keepdims=True)

    def both_of(s):
        cot = (gate_s[:, :1] * og_ref[:, piece(s)].astype(F32)).astype(BF16)
        return jnp.concatenate([tok_ref[:, piece(s)], cot], axis=0)

    def place(b):
        line = vt[b]
        slot = iota((BOTH, ROWS), 0)
        plc[b, :, :ROWS] = onehot(slot == line)
        plc[b, :, ROWS:] = onehot(slot == line + MOST)
        column = turned(line)
        lane = iota((ROWS, BOTH), 1)
        pltx[b] = onehot(lane == column)
        pltc[b] = onehot(lane == column + MOST)

    @pl.loop(0, NS)
    def _(v):
        raw[v, t] = both_of(special(v))

    pl.semaphore_wait(barrier, NZ + NQ + NT - 3)

    @pl.loop(0, NS)
    def _(v):
        rcopy(v, 0).start()
        rcopy(v, 1).start()

    for d in YD:
        vtcopy(d).start()
    place(t)

    @pl.loop(0, NN)
    def _(n):
        box[n] = dot(plc[t], both_of(normal(n))).astype(BF16).reshape(NZ, ZR, C)
        for d in ZD:
            zcopy(n, d).start()
        inz[n, z] = box[n, z]

    column, line = iota((BOTH, 1), 0), iota((1, BOTH), 1)
    across, down = iota((BOTH, BOTH), 1), iota((BOTH, BOTH), 0)
    p1[...] = onehot(source_1(column) == across)
    p1t[...] = onehot(source_1(line) == down)
    p2[...] = onehot(source_2(column) == across)
    p2t[...] = onehot(source_2(line) == down)
    for d in YD:
        vtland(d).wait_recv()
        place((t + NT - d) % NT)

    hid[...] = jnp.zeros_like(hid)
    dh[...] = jnp.zeros_like(dh)
    lg[...] = jnp.zeros_like(lg)
    own = onehot(iota((8, EXPERTS), 1) == me.astype(F32))

    @pl.loop(0, NC)
    def _(s):
        rrow[s] = dot(own, router_ref[:, piece(s)])

    def rows_of(s):
        return yb[s, :, :SLOTS, :].reshape(NT * SLOTS, C)

    def cots_of(s):
        return yb[s, :, SLOTS:, :].reshape(NT * SLOTS, C)

    def order(perm, rows, shape):
        return dot(perm[...], rows.reshape(BOTH, C)).astype(BF16).reshape(shape)

    def out_z(n):
        for d in ZD:
            zland(n, d).wait_recv()
        outx[n] = order(p1, inz[n], (NQ, XR, C))
        for d in XD:
            xcopy(n, d).start()
        inx[n, q] = outx[n, q]

    def out_x(n):
        for d in XD:
            xland(n, d).wait_recv()
        yb[normal(n), t] = order(p2, inx[n], (BOTH, C))
        ycopy(n, 0).start()
        ycopy(n, 1).start()

    def out_y(n):
        yland(n, 0).wait_recv()
        ycopy(n, 2).start()
        yland(n, 1).wait_recv()
        ycopy(n, 3).start()

    def raw_on(v):
        rland(v, 0).wait_recv()
        rcopy(v, 2).start()
        rland(v, 1).wait_recv()
        rcopy(v, 3).start()

    def unit_box(u):
        v, h = u // 2, u % 2

        @pl.when(h == 1)
        def _():
            rland(v, 2).wait_recv()
            rland(v, 3).wait_recv()

        for j in range(2):
            b = (t + 2 * h + j) % NT
            ubox[u, :, j] = dot(plc[b], raw[v, b]).astype(BF16).reshape(NZ, ZR, C)
        for d in ZD:
            uzcopy(u, d).start()
        uinz[u, z] = ubox[u, z]

    def unit_z(u):
        for d in ZD:
            uzland(u, d).wait_recv()
        for j in range(2):
            uoutx[u, :, j] = order(p1, uinz[u, :, j], (NQ, XR, C))
        for d in XD:
            uxcopy(u, d).start()
        uinx[u, q] = uoutx[u, q]

    def unit_x(u):
        for d in XD:
            uxland(u, d).wait_recv()
        v, h = u // 2, u % 2
        for j in range(2):
            yb[special(v), (t + 2 * h + j) % NT] = order(p2, uinx[u, :, j], (BOTH, C))

    def work(s):
        for copy in weights(s):
            copy.wait()
        lg[...] += dot(rows_of(s), router_ref[:, piece(s)], NTD)

        @pl.loop(0, H // N)
        def _(n):
            part = pl.ds(pl.multiple_of(n * N, N), N)
            hid[:, part] += dot(rows_of(s), wu[s, :, part])
            dh[:, part] += dot(cots_of(s), wd[s, part, :], NTD)

    def whole(n):
        yland(n, 2).wait_recv()
        yland(n, 3).wait_recv()

    @pl.loop(0, 12)
    def _(i):
        @pl.when(i < NN)
        def _():
            out_z(i)

        @pl.when(i < NS)
        def _():
            raw_on(i)

        @pl.when((i >= 1) & (i < NN + 1))
        def _():
            out_x(i - 1)

        @pl.when((i >= 1) & (i < NU + 1))
        def _():
            unit_box(i - 1)

        @pl.when((i >= 4) & (i < NU + 4))
        def _():
            unit_z(i - 4)

        @pl.when(((i >= 5) & (i < 8)) | (i == 11))
        def _():
            unit_x(i - 5 - 3 * (i // 11))

        @pl.when((i >= 4) & (i < NN + 4))
        def _():
            out_y(i - 4)

        @pl.when(i == 7)
        def _():
            whole(0)

        @pl.when(i >= 9)
        def _():
            @pl.when(i < 11)
            def _():
                whole(i - 8)

        @pl.when(i >= 7)
        def _():
            work(i - 7)

    for peers, ds in ((zpeer, ZD), (xpeer, XD)):
        for d in ds:
            pl.semaphore_signal(free, inc=1, device_id=peers(d), device_id_type=MESH)

    @pl.loop(0, NN)
    def _(n):
        for d in ZD:
            zcopy(n, d).wait_send()
        for d in XD:
            xcopy(n, d).wait_send()
        for i in range(4):
            ycopy(n, i).wait_send()

    @pl.loop(0, NU)
    def _(u):
        for d in ZD:
            uzcopy(u, d).wait_send()
        for d in XD:
            uxcopy(u, d).wait_send()

    @pl.loop(0, NS)
    def _(v):
        for i in range(4):
            rcopy(v, i).wait_send()

    BR = 32

    @pl.loop(0, NT * SLOTS // BR)
    def _(b):
        r = pl.ds(pl.multiple_of(b * BR, BR), BR)
        v, back = hid[r, :], dh[r, :]
        sig = 1.0 / (1.0 + jnp.exp(-v))
        a = (v * sig).astype(BF16)
        act[r, :] = a
        hc[r, :] = (back * (sig * (1.0 + v * (1.0 - sig)))).astype(BF16)
        part = jnp.sum(a.astype(F32) * back, axis=1, keepdims=True)
        mine = iota((BR, EXPERTS), 1) == me.astype(F32)
        logit = jnp.sum(jnp.where(mine, lg[r, :], 0.0), axis=1, keepdims=True)
        slope = part * (1.0 - 1.0 / (1.0 + jnp.exp(-logit)))
        slope_s[r, :] = jnp.broadcast_to(slope, (BR, 128))
        s1 = slope.astype(BF16).astype(F32)
        s2 = (slope - s1).astype(BF16).astype(F32)
        s3 = slope - s1 - s2
        k = iota((BR, 128), 1)
        slope3[r, :] = jnp.where(
            k == 0.0, s1, jnp.where(k == 1.0, s2, jnp.where(k == 2.0, s3, 0.0))
        ).astype(BF16)

    pl.semaphore_wait(free, NZ + NQ - 2)

    def partial(s, b):
        r = pl.ds(pl.multiple_of(b * SLOTS, SLOTS), SLOTS)
        value = dot(act[r, :], wd[s])
        grad = dot(hc[r, :], wu[s], NTD) + slope_s[r, :1] * rrow[s, :1, :]
        return value, grad

    def back_far(n):
        value, grad = partial(normal(n), far)
        sa[n, 0] = value.astype(BF16)
        sa[n, 1] = grad.astype(BF16)
        acopy(n, 0).start()
        acopy(n, 1).start()

    def back_near(n):
        value, grad = partial(normal(n), right)
        acopy(n, 0).wait_recv()
        sb[n, 0, lo] = (value + ra[n, 0].astype(F32)).astype(BF16)
        sb[n, 0, hi] = grad.astype(BF16)
        bcopy(n, 0).start()
        value, grad = partial(normal(n), left)
        acopy(n, 1).wait_recv()
        sb[n, 1, lo] = value.astype(BF16)
        sb[n, 1, hi] = (grad + ra[n, 1].astype(F32)).astype(BF16)
        bcopy(n, 1).start()

    def back_own(n):
        value, grad = partial(normal(n), t)
        bcopy(n, 0).wait_recv()
        bcopy(n, 1).wait_recv()
        value = value + rb[n, 0, :SLOTS, :].astype(F32) + rb[n, 1, :SLOTS, :].astype(F32)
        grad = grad + rb[n, 0, SLOTS:, :].astype(F32) + rb[n, 1, SLOTS:, :].astype(F32)
        both = jnp.concatenate([value, grad], axis=0).astype(BF16)
        outx[n] = order(p2t, both, (NQ, XR, C))
        for d in XD:
            xcopy(n, d).start()
        inx[n, q] = outx[n, q]

    def back_x(n):
        for d in XD:
            xland(n, d).wait_recv()
        box[n] = order(p1t, inx[n], (NZ, ZR, C))
        for d in ZD:
            zcopy(n, d).start()
        inz[n, z] = box[n, z]

    def back_z(n):
        for d in ZD:
            zland(n, d).wait_recv()
        got = inz[n].reshape(BOTH, C)
        cols = piece(normal(n))
        mixed_ref[:, cols] = (gate_s[:, :1] * dot(pltx[t], got)).astype(BF16)
        tgrad_ref[:, cols] = dot(pltc[t], got).astype(BF16)

    def unit_back(u):
        v, h = u // 2, 1 - u % 2
        for j in range(2):
            value, grad = partial(special(v), (t + 2 * h + j) % NT)
            both = jnp.concatenate([value, grad], axis=0).astype(BF16)
            uoutx[u, :, j] = order(p2t, both, (NQ, XR, C))
        for d in XD:
            uxcopy(u, d).start()
        uinx[u, q] = uoutx[u, q]

    def unit_back_x(u):
        for d in XD:
            uxland(u, d).wait_recv()
        for j in range(2):
            ubox[u, :, j] = order(p1t, uinx[u, :, j], (NZ, ZR, C))
        for d in ZD:
            uzcopy(u, d).start()
        uinz[u, z] = ubox[u, z]

    def unit_back_z(u):
        for d in ZD:
            uzland(u, d).wait_recv()
        v, h = u // 2, 1 - u % 2
        for j in range(2):
            o = 2 * h + j
            b = (t + o) % NT
            got = uinz[u, :, j].reshape(BOTH, C)
            raw[v, o, rlo] = dot(pltx[b], got).astype(BF16)
            raw[v, o, rhi] = dot(pltc[b], got).astype(BF16)

        @pl.when(h == 1)
        def _():
            uacopy(v, 0).start()
            uacopy(v, 1).start()

        @pl.when(h == 0)
        def _():
            uacopy(v, 0).wait_recv()
            raw[v, 1, rlo] = (raw[v, 1, rlo].astype(F32) + ua[v, 0].astype(F32)).astype(BF16)
            ubcopy(v, 0).start()
            uacopy(v, 1).wait_recv()
            raw[v, 3, rhi] = (raw[v, 3, rhi].astype(F32) + ua[v, 1].astype(F32)).astype(BF16)
            ubcopy(v, 1).start()

    def unit_sum(v):
        ubcopy(v, 0).wait_recv()
        ubcopy(v, 1).wait_recv()
        got = raw[v, 0].astype(F32) + ub[v, 0].astype(F32) + ub[v, 1].astype(F32)
        cols = piece(special(v))
        value = got[:ROWS].astype(BF16).astype(F32)
        mixed_ref[:, cols] = (gate_s[:, :1] * value).astype(BF16)
        tgrad_ref[:, cols] = got[ROWS:].astype(BF16)

    def grads_out(s, n):
        part = pl.ds(pl.multiple_of(n * N, N), N)
        k = n % 2
        return (
            pltpu.make_async_copy(gsu.at[k], upg_hbm.at[0, piece(s), part], gsem.at[0, k]),
            pltpu.make_async_copy(gsd.at[k], downg_hbm.at[0, part, piece(s)], gsem.at[1, k]),
        )

    def grads(s):
        @pl.loop(0, H // N)
        def _(n):
            @pl.when((s > 0) | (n >= 2))
            def _():
                for copy in grads_out(s, n):
                    copy.wait()

            part = pl.ds(pl.multiple_of(n * N, N), N)
            gsd[n % 2] = dot(act[:, part], cots_of(s), TND).astype(BF16)
            gsu[n % 2] = dot(rows_of(s), hc[:, part], TND).astype(BF16)
            for copy in grads_out(s, n):
                copy.start()

    def vector_0():
        @pl.loop(0, NC)
        def _(s):
            three = dot(slope3[...], rows_of(s), TND)
            vy[t, :, piece(s)] = jnp.sum(three, axis=0, keepdims=True)

        for d in YD:
            vycopy(d).start()

    def vector_1():
        for d in YD:
            vyland(d).wait_recv()
        vx[q] = (vy[0] + vy[1]) + (vy[2] + vy[3])
        for d in XD:
            vxcopy(d).start()

    def vector_2():
        for d in XD:
            vxland(d).wait_recv()
        for d in ZD:
            vzcopy(d).start()
        vz[z] = vx[...]

    @pl.loop(0, 10)
    def _(j):
        @pl.when(j < NN)
        def _():
            back_far(j)

        @pl.when((j >= 1) & (j < NN + 1))
        def _():
            back_near(j - 1)

        @pl.when(j < NU)
        def _():
            unit_back(j)

        @pl.when(j == 3)
        def _():
            vector_0()

        @pl.when(j == 5)
        def _():
            vector_1()

        @pl.when(j == 7)
        def _():
            vector_2()

        @pl.when((j >= 3) & (j < NU + 3))
        def _():
            unit_back_x(j - 3)

        @pl.when((j >= 4) & (j < NU + 4))
        def _():
            unit_back_z(j - 4)

        @pl.when((j >= 4) & (j < NC + 4))
        def _():
            grads(j - 4)

        @pl.when((j >= 3) & (j < NN + 3))
        def _():
            back_own(j - 3)

        @pl.when((j >= 4) & (j < NN + 4))
        def _():
            back_x(j - 4)

        @pl.when((j >= 5) & (j < NN + 5))
        def _():
            back_z(j - 5)

        @pl.when(j >= 8)
        def _():
            unit_sum(j - 8)

    for d in ZD:
        vzland(d).wait_recv()
    rgrad_ref[...] = vz[...].reshape(EXPERTS, 1, C * NC)
    for d in YD:
        vtcopy(d).wait_send()
        vycopy(d).wait_send()
    for d in XD:
        vxcopy(d).wait_send()
    for d in ZD:
        vzcopy(d).wait_send()

    @pl.loop(0, NN)
    def _(n):
        for i in range(2):
            acopy(n, i).wait_send()
            bcopy(n, i).wait_send()
        for d in XD:
            xcopy(n, d).wait_send()
        for d in ZD:
            zcopy(n, d).wait_send()

    @pl.loop(0, NU)
    def _(u):
        for d in XD:
            uxcopy(u, d).wait_send()
        for d in ZD:
            uzcopy(u, d).wait_send()

    @pl.loop(0, NS)
    def _(v):
        for i in range(2):
            uacopy(v, i).wait_send()
            ubcopy(v, i).wait_send()

    for n in range(2):
        for copy in grads_out(NC - 1, n):
            copy.wait()


def per_device(tokens, expert_ids, live_counts, router, up_weight, down_weight, out_grad):
    width = tokens.shape[1]
    assert tokens.shape == (ROWS, C * NC) and router.shape[1] == EXPERTS
    assert up_weight.shape == (1, C * NC, H)
    vmem = pl.BlockSpec(memory_space=pltpu.VMEM)
    smem = pl.BlockSpec(memory_space=pltpu.SMEM)
    hbm = pl.BlockSpec(memory_space=pl.ANY)
    every = NT * SLOTS
    V, DMA = pltpu.VMEM, pltpu.SemaphoreType.DMA
    scratch = [
        V((NN, NZ, ZR, C), BF16),
        V((NN, NZ, ZR, C), BF16),
        V((NN, NQ, XR, C), BF16),
        V((NN, NQ, XR, C), BF16),
        V((NU, NZ, 2, ZR, C), BF16),
        V((NU, NZ, 2, ZR, C), BF16),
        V((NU, NQ, 2, XR, C), BF16),
        V((NU, NQ, 2, XR, C), BF16),
        V((NS, NT, 2 * ROWS, C), BF16),
        V((NC, NT, BOTH, C), BF16),
        V((NC, C, H), BF16),
        V((NC, H, C), BF16),
        V((every, H), F32),
        V((every, H), F32),
        V((every, H), BF16),
        V((every, H), BF16),
        V((every, EXPERTS), F32),
        V((ROWS, 128), F32),
        V((every, 128), F32),
        V((every, 128), BF16),
        V((NN, 2, SLOTS, C), BF16),
        V((NN, 2, SLOTS, C), BF16),
        V((NN, 2, BOTH, C), BF16),
        V((NN, 2, BOTH, C), BF16),
        V((NS, 2, ROWS, C), BF16),
        V((NS, 2, 2 * ROWS, C), BF16),
        V((2, C, N), BF16),
        V((2, N, C), BF16),
        V((BOTH, BOTH), BF16),
        V((BOTH, BOTH), BF16),
        V((BOTH, BOTH), BF16),
        V((BOTH, BOTH), BF16),
        V((NT, BOTH, 2 * ROWS), BF16),
        V((NT, ROWS, BOTH), BF16),
        V((NT, ROWS, BOTH), BF16),
        V((NC, 8, C), F32),
        V((NT, 1, ROWS), F32),
        V((NT, 1, width), F32),
        V((NQ, 1, width), F32),
        V((NZ, NQ, 1, width), F32),
        DMA((2, NC)),
        DMA((NN, NZ)), DMA((NN, NZ)), DMA((NN, NQ)), DMA((NN, NQ)), DMA((NN, 4)), DMA((NN, 4)),
        DMA((NN, 2)), DMA((NN, 2)), DMA((NN, 2)), DMA((NN, 2)),
        DMA((NU, NZ)), DMA((NU, NZ)), DMA((NU, NQ)), DMA((NU, NQ)), DMA((NS, 4)), DMA((NS, 4)),
        DMA((NS, 2)), DMA((NS, 2)), DMA((NS, 2)), DMA((NS, 2)),
        DMA((2, 2)),
        DMA((NT,)), DMA((NT,)), DMA((NT,)), DMA((NT,)),
        DMA((NQ,)), DMA((NQ,)), DMA((NZ,)), DMA((NZ,)),
        pltpu.SemaphoreType.REGULAR,
    ]
    S = jax.ShapeDtypeStruct
    mixed, tgrad, upg, downg, rgrad = pl.pallas_call(
        kernel,
        out_shape=(
            S((ROWS, width), BF16),
            S((ROWS, width), BF16),
            S((1, width, H), BF16),
            S((1, H, width), BF16),
            S((EXPERTS, 1, width), F32),
        ),
        in_specs=[vmem, smem, vmem, vmem, vmem, hbm, hbm],
        out_specs=(vmem, vmem, hbm, hbm, vmem),
        scratch_shapes=scratch,
        compiler_params=pltpu.CompilerParams(
            collective_id=0, has_side_effects=True, vmem_limit_bytes=67043328
        ),
    )(
        expert_ids.reshape(1, ROWS), live_counts, router.T, tokens, out_grad, up_weight, down_weight
    )
    return (mixed, tgrad, upg, downg, rgrad.reshape(EXPERTS, width).T)


def solution(mesh):
    rows = P(("expert", "tensor"), None)
    in_specs = (
        rows,
        rows,
        P(("expert", "tensor")),
        P(),
        P("expert", None, "tensor"),
        P("expert", "tensor", None),
        rows,
    )
    out_specs = (rows, rows, P("expert", None, "tensor"), P("expert", "tensor", None), P())
    return jax.shard_map(
        per_device, mesh=mesh, in_specs=in_specs, out_specs=out_specs, check_vma=False
    )
```

time: 202 us -> 193 us (0.955)
  Pallas kernels: 183 us -> 177 us
  local copies, waits for them, and re-layouts: 17.1 us -> 13.7 us
    pallas_call x1, Pallas kernels: 183 us -> 177 us  [per_device(): pl.pallas_call(kernel, out_shape=(S((ROWS, width), BF16), S((ROWS, width)...]
    unnamed x11 -> x9, local copies, waits for them, and re-layouts: 17.1 us -> 13.7 us
where the time goes in v3:
time: 193 us; the launch traced here: 192 us
  Pallas kernels  177 us (92%)
  local copies, waits for them, and re-layouts  13.7 us (7%)
    pallas_call x1, Pallas kernels, per_device(): pl.pallas_call(kernel, out_shape=(S((ROWS, width), BF16), S((ROWS, width)...  177 us
    unnamed x9, local copies, waits for them, and re-layouts  13.7 us

profile of v3, /device:TPU:1, one launch (start us, length us, event | category | flops | bytes accessed | tf_op | source)
XLA Modules:
  0.0 192.4 jit_solution(17466393112786337468)
XLA Ops:
  1.3 177.4 %shard_map.110 = (bf16[128,2560]{1,0:T(8,128)(2,1)}, bf16[128,2560]{1,0:T(8,128)(2,1)}, bf16[1,2560,1024]{2,1,0:T(8,128)(2,1)}, bf16[1,1024,2560]{2,1,0:T(8,128)(2,1)}, f32[32,1,2560]{2,1,0:T(1,128)}) custom-call(s32[1,128]{1,0:T(1,128)} %bitcast.11, s32[1]{0:T(128)S(6)} %copy.19.live_ref, bf16[32,2560]{1,0:T(8,128)(2,1)} %bitcast.10, ...), custom_call_target="tpu_custom_call" | custom-call | tf_op jit(solution)/shard_map/pallas_call | solution.py:755
  178.7 1.7 copy.14
  180.4 2.0 %copy.20 = bf16[128,2560]{1,0:T(8,128)(2,1)} copy(bf16[128,2560]{1,0:T(8,128)(2,1)} %get-tuple-element.20) | data formatting | bytes 1310720
  182.4 0.0 slice-start
  182.4 2.1 %copy.21 = bf16[128,2560]{1,0:T(8,128)(2,1)} copy(bf16[128,2560]{1,0:T(8,128)(2,1)} %get-tuple-element.21) | data formatting | bytes 1310720
  184.5 0.0 slice-start.1
  184.5 5.5 %copy.22 = bf16[1,2560,1024]{2,1,0:T(8,128)(2,1)} copy(bf16[1,2560,1024]{2,1,0:T(8,128)(2,1)} %get-tuple-element.22) | data formatting | bytes 10485760
  190.0 0.0 slice-done
  190.0 0.0 slice-done.1
  190.0 2.4 %copy.23 = bf16[1,1024,2560]{2,1,0:T(8,128)(2,1)} copy(bf16[1,1024,2560]{2,1,0:T(8,128)(2,1)S(1)} %bitcast.8) | data formatting | bytes 10485760
  (1 shorter events, 0.0 us)
Async XLA Ops:
  182.4 7.6 %slice-start = ((s8[5242880]{0:T(1024)(128)(4,1)}), s8[4194304]{0:T(1024)(128)(4,1)S(1)}, s32[]{:S(2)}) async-start(s8[5242880]{0:T(1024)(128)(4,1)} %bitcast.7), calls=%async_computation | async-start | bytes 8388608
  184.5 5.5 %slice-start.1 = ((s8[5242880]{0:T(1024)(128)(4,1)}), s8[1048576]{0:T(1024)(128)(4,1)S(1)}, s32[]{:S(2)}) async-start(s8[5242880]{0:T(1024)(128)(4,1)} %bitcast.7), calls=%async_computation.1 | async-start | bytes 2097152

commit v4 on v3

--- a/solution.py
+++ b/solution.py
@@ -15,12 +15,44 @@
 BOTH = 2 * SLOTS
 C, NC = 512, 5
 NN, NS = 3, 2
-NU = 2 * NS
+NU = NT * NS
 ZR, XR = NQ * 2 * MOST, 2 * NZ * MOST
 H = 1024
 N = 256
 
 
+OUT_STEPS = 22
+OUT = dict(
+    out_z=(1, 3, 4,),
+    raw_on=(1, 3,),
+    unit_box=(0, 1, 2, 4, 5, 6, 7, 8,),
+    out_x=(3, 7, 9,),
+    unit_z=(8, 9, 10, 11, 12, 13, 14, 15,),
+    unit_x=(9, 10, 11, 12, 13, 14, 16, 19,),
+    release=(19,),
+    out_y=(9, 11, 13,),
+    near=(9, 10, 11, 13, 14,),
+    away=(16, 17, 18, 19, 20,),
+    middle=(14, 15, 20, 21,),
+)
+BACK_STEPS = 28
+BACK = dict(
+    back_far=(0, 1, 2,),
+    unit_back=(2, 3, 4, 5, 6, 7, 8, 9,),
+    vector_0=(9,),
+    back_near=(9, 10, 11,),
+    unit_back_x=(8, 9, 11, 12, 13, 15, 16, 20,),
+    unit_back_z=(10, 16, 17, 18, 19, 23, 24, 25,),
+    grads=(11, 12, 13, 14, 15,),
+    back_own=(12, 15, 21,),
+    vector_1=(12,),
+    vector_2=(15,),
+    back_x=(20, 21, 22,),
+    unit_sum=(21, 27,),
+    back_z=(21, 25, 26,),
+)
+
+
 def dot(a, b, dims=((1,), (0,))):
     return lax.dot_general(a, b, (dims, ((), ())), preferred_element_type=F32)
 
@@ -31,6 +63,21 @@
 
 def iota(shape, axis):
     return lax.broadcasted_iota(I32, shape, axis).astype(F32)
+
+
+def gray(r):
+    return r + r // 2 - 2 * (r // 3)
+
+
+def at(i, steps, task):
+    here, k = i == steps[0], 0
+    for step in steps[1:]:
+        here = here | (i == step)
+        k = k + (i + 64 - step) // 64
+
+    @pl.when(here)
+    def _():
+        task(k)
 
 
 def onehot(mask):
@@ -71,7 +118,6 @@
     me = lax.axis_index("expert")
     t = lax.axis_index("tensor")
     z, q = me // NQ, me % NQ
-    left, right, far = (t + NT - 1) % NT, (t + 1) % NT, (t + 2) % NT
     lo, hi = pl.ds(0, SLOTS), pl.ds(SLOTS, SLOTS)
     rlo, rhi = pl.ds(0, ROWS), pl.ds(ROWS, ROWS)
     ZD, XD, YD = range(1, NZ), range(1, NQ), range(1, NT)
@@ -133,22 +179,16 @@
     SIDE = (1, NT - 1, 1, NT - 1)
 
     def ycopy(n, i):
-        s = normal(n)
-        src = (yb.at[s, t], yb.at[s, t], yb.at[s, left, lo], yb.at[s, right, hi])[i]
-        return remote(src, src, ys.at[n, i], yr.at[n, i], ypeer(SIDE[i]))
-
-    def yland(n, i):
-        s = normal(n)
-        dst = (yb.at[s, left], yb.at[s, right], yb.at[s, far, lo], yb.at[s, far, hi])[i]
-        return remote(dst, dst, ys.at[n, i], yr.at[n, i], ypeer(SIDE[i]))
+        b = yb.at[normal(n)]
+        src = (b.at[0], b.at[0], b.at[3, lo], b.at[1, hi])[i]
+        dst = (b.at[3], b.at[1], b.at[2, lo], b.at[2, hi])[i]
+        return remote(src, dst, ys.at[n, i], yr.at[n, i], ypeer(SIDE[i]))
 
     def rcopy(v, i):
-        src = (raw.at[v, t], raw.at[v, t], raw.at[v, left, rlo], raw.at[v, right, rhi])[i]
-        return remote(src, src, rs.at[v, i], rr.at[v, i], ypeer(SIDE[i]))
-
-    def rland(v, i):
-        dst = (raw.at[v, left], raw.at[v, right], raw.at[v, far, rlo], raw.at[v, far, rhi])[i]
-        return remote(dst, dst, rs.at[v, i], rr.at[v, i], ypeer(SIDE[i]))
+        b = raw.at[v]
+        src = (b.at[0], b.at[0], b.at[3, rlo], b.at[1, rhi])[i]
+        dst = (b.at[3], b.at[1], b.at[2, rlo], b.at[2, rhi])[i]
+        return remote(src, dst, rs.at[v, i], rr.at[v, i], ypeer(SIDE[i]))
 
     def acopy(n, i):
         return remote(sa.at[n, i], ra.at[n, i], as_.at[n, i], ar.at[n, i], ypeer(SIDE[i]))
@@ -164,11 +204,7 @@
         return remote(raw.at[v, SIDE[i]], ub.at[v, i], ubs.at[v, i], ubr.at[v, i], ypeer(SIDE[i]))
 
     def vtcopy(d):
-        return remote(vt.at[t], vt.at[t], vts.at[d], vtr.at[d], ypeer(d))
-
-    def vtland(d):
-        dst = vt.at[(t + NT - d) % NT]
-        return remote(dst, dst, vts.at[d], vtr.at[d], ypeer(d))
+        return remote(vt.at[0], vt.at[NT - d], vts.at[d], vtr.at[d], ypeer(d))
 
     def vycopy(d):
         return remote(vy.at[t], vy.at[t], vys.at[d], vyr.at[d], ypeer(d))
@@ -204,50 +240,46 @@
     def turned(line):
         return jnp.sum(jnp.where(diag, line, 0.0), axis=1, keepdims=True)
 
+    def both_of(s):
+        cot = (gate_s[:, :1] * og_ref[:, piece(s)].astype(F32)).astype(BF16)
+        return jnp.concatenate([tok_ref[:, piece(s)], cot], axis=0)
+
+    def place(o):
+        line = vt[o]
+        slot = iota((BOTH, ROWS), 0)
+        plc[o, :, :ROWS] = onehot(slot == line)
+        plc[o, :, ROWS:] = onehot(slot == line + MOST)
+        column = turned(line)
+        lane = iota((ROWS, BOTH), 1)
+        pltx[o] = onehot(lane == column)
+        pltc[o] = onehot(lane == column + MOST)
+
     ids = turned(ids_ref[...].astype(F32))
     chosen = ids == iota((ROWS, EXPERTS), 1)
+    logits = dot(tok_ref[...], router_ref[...], NTD)
+    gate = jax.nn.sigmoid(jnp.sum(jnp.where(chosen, logits, 0.0), axis=1, keepdims=True))
+    gate_s[...] = jnp.broadcast_to(gate, (ROWS, 128))
+    raw[0, 0] = both_of(special(0))
+    pl.semaphore_wait(barrier, NZ + NQ + NT - 3)
+    rcopy(0, 0).start()
+    rcopy(0, 1).start()
+
     tri = onehot(iota((ROWS, ROWS), 0) > iota((ROWS, ROWS), 1))
     counts = dot(tri, onehot(chosen))
     rank = jnp.sum(jnp.where(chosen, counts, 0.0), axis=1, keepdims=True)
-    logits = dot(tok_ref[...], router_ref[...], NTD)
-    gate = jax.nn.sigmoid(jnp.sum(jnp.where(chosen, logits, 0.0), axis=1, keepdims=True))
-    gate_s[...] = jnp.broadcast_to(gate, (ROWS, 128))
     live = lax.broadcasted_iota(I32, (ROWS, 1), 0) < live_ref[0]
     target = jnp.where(live, ids * (2.0 * MOST) + rank, -1000.0)
-    vt[t] = jnp.sum(jnp.where(diag, target, 0.0), axis=0, keepdims=True)
-
-    def both_of(s):
-        cot = (gate_s[:, :1] * og_ref[:, piece(s)].astype(F32)).astype(BF16)
-        return jnp.concatenate([tok_ref[:, piece(s)], cot], axis=0)
-
-    def place(b):
-        line = vt[b]
-        slot = iota((BOTH, ROWS), 0)
-        plc[b, :, :ROWS] = onehot(slot == line)
-        plc[b, :, ROWS:] = onehot(slot == line + MOST)
-        column = turned(line)
-        lane = iota((ROWS, BOTH), 1)
-        pltx[b] = onehot(lane == column)
-        pltc[b] = onehot(lane == column + MOST)
-
-    @pl.loop(0, NS)
-    def _(v):
-        raw[v, t] = both_of(special(v))
-
-    pl.semaphore_wait(barrier, NZ + NQ + NT - 3)
-
-    @pl.loop(0, NS)
-    def _(v):
-        rcopy(v, 0).start()
-        rcopy(v, 1).start()
-
+    vt[0] = jnp.sum(jnp.where(diag, target, 0.0), axis=0, keepdims=True)
+    raw[1, 0] = both_of(special(1))
     for d in YD:
         vtcopy(d).start()
-    place(t)
+    rcopy(1, 0).start()
+    rcopy(1, 1).start()
+    place(0)
 
     @pl.loop(0, NN)
     def _(n):
-        box[n] = dot(plc[t], both_of(normal(n))).astype(BF16).reshape(NZ, ZR, C)
+        box[n] = dot(plc[0], both_of(normal(n))).astype(BF16).reshape(NZ, ZR, C)
         for d in ZD:
             zcopy(n, d).start()
         inz[n, z] = box[n, z]
@@ -259,8 +291,8 @@
     p2[...] = onehot(source_2(column) == across)
     p2t[...] = onehot(source_2(line) == down)
     for d in YD:
-        vtland(d).wait_recv()
-        place((t + NT - d) % NT)
+        vtcopy(d).wait_recv()
+        place(NT - d)
 
     hid[...] = jnp.zeros_like(hid)
     dh[...] = jnp.zeros_like(dh)
@@ -291,33 +323,32 @@
     def out_x(n):
         for d in XD:
             xland(n, d).wait_recv()
-        yb[normal(n), t] = order(p2, inx[n], (BOTH, C))
+        yb[normal(n), 0] = order(p2, inx[n], (BOTH, C))
         ycopy(n, 0).start()
         ycopy(n, 1).start()
 
     def out_y(n):
-        yland(n, 0).wait_recv()
+        ycopy(n, 0).wait_recv()
         ycopy(n, 2).start()
-        yland(n, 1).wait_recv()
+        ycopy(n, 1).wait_recv()
         ycopy(n, 3).start()
 
     def raw_on(v):
-        rland(v, 0).wait_recv()
+        rcopy(v, 0).wait_recv()
         rcopy(v, 2).start()
-        rland(v, 1).wait_recv()
+        rcopy(v, 1).wait_recv()
         rcopy(v, 3).start()
 
     def unit_box(u):
-        v, h = u // 2, u % 2
-
-        @pl.when(h == 1)
+        v, r = u // NT, u % NT
+
+        @pl.when(r == 3)
         def _():
-            rland(v, 2).wait_recv()
-            rland(v, 3).wait_recv()
-
-        for j in range(2):
-            b = (t + 2 * h + j) % NT
-            ubox[u, :, j] = dot(plc[b], raw[v, b]).astype(BF16).reshape(NZ, ZR, C)
+            rcopy(v, 2).wait_recv()
+            rcopy(v, 3).wait_recv()
+
+        o = gray(r)
+        ubox[u] = dot(plc[o], raw[v, o]).astype(BF16).reshape(NZ, ZR, C)
         for d in ZD:
             uzcopy(u, d).start()
         uinz[u, z] = ubox[u, z]
@@ -325,8 +356,7 @@
     def unit_z(u):
         for d in ZD:
             uzland(u, d).wait_recv()
-        for j in range(2):
-            uoutx[u, :, j] = order(p1, uinz[u, :, j], (NQ, XR, C))
+        uoutx[u] = order(p1, uinz[u], (NQ, XR, C))
         for d in XD:
             uxcopy(u, d).start()
         uinx[u, q] = uoutx[u, q]
@@ -334,99 +364,50 @@
     def unit_x(u):
         for d in XD:
             uxland(u, d).wait_recv()
-        v, h = u // 2, u % 2
-        for j in range(2):
-            yb[special(v), (t + 2 * h + j) % NT] = order(p2, uinx[u, :, j], (BOTH, C))
-
-    def work(s):
-        for copy in weights(s):
-            copy.wait()
-        lg[...] += dot(rows_of(s), router_ref[:, piece(s)], NTD)
+        yb[special(u // NT), gray(u % NT)] = order(p2, uinx[u], (BOTH, C))
+
+    def release(_):
+        for peers, ds in ((zpeer, ZD), (xpeer, XD)):
+            for d in ds:
+                pl.semaphore_signal(free, inc=1, device_id=peers(d), device_id_type=MESH)
+
+    HALF = 2 * SLOTS
+
+    def work(s, h):
+        r = pl.ds(h * HALF, HALF)
+        rows = yb[s, 2 * h : 2 * h + 2, :SLOTS, :].reshape(HALF, C)
+        cots = yb[s, 2 * h : 2 * h + 2, SLOTS:, :].reshape(HALF, C)
+        lg[r, :] += dot(rows, router_ref[:, piece(s)], NTD)
 
         @pl.loop(0, H // N)
         def _(n):
             part = pl.ds(pl.multiple_of(n * N, N), N)
-            hid[:, part] += dot(rows_of(s), wu[s, :, part])
-            dh[:, part] += dot(cots_of(s), wd[s, part, :], NTD)
-
-    def whole(n):
-        yland(n, 2).wait_recv()
-        yland(n, 3).wait_recv()
-
-    @pl.loop(0, 12)
-    def _(i):
-        @pl.when(i < NN)
-        def _():
-            out_z(i)
-
-        @pl.when(i < NS)
-        def _():
-            raw_on(i)
-
-        @pl.when((i >= 1) & (i < NN + 1))
-        def _():
-            out_x(i - 1)
-
-        @pl.when((i >= 1) & (i < NU + 1))
-        def _():
-            unit_box(i - 1)
-
-        @pl.when((i >= 4) & (i < NU + 4))
-        def _():
-            unit_z(i - 4)
-
-        @pl.when(((i >= 5) & (i < 8)) | (i == 11))
-        def _():
-            unit_x(i - 5 - 3 * (i // 11))
-
-        @pl.when((i >= 4) & (i < NN + 4))
-        def _():
-            out_y(i - 4)
-
-        @pl.when(i == 7)
-        def _():
-            whole(0)
-
-        @pl.when(i >= 9)
-        def _():
-            @pl.when(i < 11)
+            hid[r, part] += dot(rows, wu[s, :, part])
+            dh[r, part] += dot(cots, wd[s, part, :], NTD)
+
+    def near(s):
+        for copy in weights(s):
+            copy.wait()
+        work(s, 0)
+
+    def away(s):
+        for n in range(NN):
+
+            @pl.when(s == normal(n))
             def _():
-                whole(i - 8)
-
-        @pl.when(i >= 7)
-        def _():
-            work(i - 7)
-
-    for peers, ds in ((zpeer, ZD), (xpeer, XD)):
-        for d in ds:
-            pl.semaphore_signal(free, inc=1, device_id=peers(d), device_id_type=MESH)
-
-    @pl.loop(0, NN)
-    def _(n):
-        for d in ZD:
-            zcopy(n, d).wait_send()
-        for d in XD:
-            xcopy(n, d).wait_send()
-        for i in range(4):
-            ycopy(n, i).wait_send()
-
-    @pl.loop(0, NU)
-    def _(u):
-        for d in ZD:
-            uzcopy(u, d).wait_send()
-        for d in XD:
-            uxcopy(u, d).wait_send()
-
-    @pl.loop(0, NS)
-    def _(v):
-        for i in range(4):
-            rcopy(v, i).wait_send()
+                ycopy(n, 2).wait_recv()
+                ycopy(n, 3).wait_recv()
+
+        work(s, 1)
 
     BR = 32
 
-    @pl.loop(0, NT * SLOTS // BR)
-    def _(b):
-        r = pl.ds(pl.multiple_of(b * BR, BR), BR)
+    def middle(o):
+        @pl.loop(0, SLOTS // BR)
+        def _(b):
+            silu_rows(pl.ds(pl.multiple_of(o * SLOTS + b * BR, BR), BR))
+
+    def silu_rows(r):
         v, back = hid[r, :], dh[r, :]
         sig = 1.0 / (1.0 + jnp.exp(-v))
         a = (v * sig).astype(BF16)
@@ -445,7 +426,10 @@
             k == 0.0, s1, jnp.where(k == 1.0, s2, jnp.where(k == 2.0, s3, 0.0))
         ).astype(BF16)
 
-    pl.semaphore_wait(free, NZ + NQ - 2)
+    @pl.loop(0, OUT_STEPS)
+    def _(i):
+        for task in (out_z, raw_on, unit_box, out_x, unit_z, unit_x, release, out_y, near, away, middle):
+            at(i, OUT[task.__name__], task)
 
     def partial(s, b):
         r = pl.ds(pl.multiple_of(b * SLOTS, SLOTS), SLOTS)
@@ -454,31 +438,33 @@
         return value, grad
 
     def back_far(n):
-        value, grad = partial(normal(n), far)
+        value, grad = partial(normal(n), 2)
         sa[n, 0] = value.astype(BF16)
         sa[n, 1] = grad.astype(BF16)
         acopy(n, 0).start()
         acopy(n, 1).start()
 
     def back_near(n):
-        value, grad = partial(normal(n), right)
+        value, grad = partial(normal(n), 1)
         acopy(n, 0).wait_recv()
         sb[n, 0, lo] = (value + ra[n, 0].astype(F32)).astype(BF16)
         sb[n, 0, hi] = grad.astype(BF16)
         bcopy(n, 0).start()
-        value, grad = partial(normal(n), left)
+        value, grad = partial(normal(n), 3)
         acopy(n, 1).wait_recv()
         sb[n, 1, lo] = value.astype(BF16)
         sb[n, 1, hi] = (grad + ra[n, 1].astype(F32)).astype(BF16)
         bcopy(n, 1).start()
 
     def back_own(n):
-        value, grad = partial(normal(n), t)
+        value, grad = partial(normal(n), 0)
         bcopy(n, 0).wait_recv()
         bcopy(n, 1).wait_recv()
         value = value + rb[n, 0, :SLOTS, :].astype(F32) + rb[n, 1, :SLOTS, :].astype(F32)
         grad = grad + rb[n, 0, SLOTS:, :].astype(F32) + rb[n, 1, SLOTS:, :].astype(F32)
         both = jnp.concatenate([value, grad], axis=0).astype(BF16)
+        for d in XD:
+            xcopy(n, d).wait_send()
         outx[n] = order(p2t, both, (NQ, XR, C))
         for d in XD:
             xcopy(n, d).start()
@@ -487,6 +473,8 @@
     def back_x(n):
         for d in XD:
             xland(n, d).wait_recv()
+        for d in ZD:
+            zcopy(n, d).wait_send()
         box[n] = order(p1t, inx[n], (NZ, ZR, C))
         for d in ZD:
             zcopy(n, d).start()
@@ -497,15 +485,20 @@
             zland(n, d).wait_recv()
         got = inz[n].reshape(BOTH, C)
         cols = piece(normal(n))
-        mixed_ref[:, cols] = (gate_s[:, :1] * dot(pltx[t], got)).astype(BF16)
-        tgrad_ref[:, cols] = dot(pltc[t], got).astype(BF16)
+        mixed_ref[:, cols] = (gate_s[:, :1] * dot(pltx[0], got)).astype(BF16)
+        tgrad_ref[:, cols] = dot(pltc[0], got).astype(BF16)
 
     def unit_back(u):
-        v, h = u // 2, 1 - u % 2
-        for j in range(2):
-            value, grad = partial(special(v), (t + 2 * h + j) % NT)
-            both = jnp.concatenate([value, grad], axis=0).astype(BF16)
-            uoutx[u, :, j] = order(p2t, both, (NQ, XR, C))
+        value, grad = partial(special(u // NT), gray(3 - u % NT))
+        both = jnp.concatenate([value, grad], axis=0).astype(BF16)
+        for d in XD:
+            uxcopy(u, d).wait_send()
+        uoutx[u] = order(p2t, both, (NQ, XR, C))
+
+        @pl.when(u == 0)
+        def _():
+            pl.semaphore_wait(free, NZ + NQ - 2)
+
         for d in XD:
             uxcopy(u, d).start()
         uinx[u, q] = uoutx[u, q]
@@ -513,8 +506,9 @@
     def unit_back_x(u):
         for d in XD:
             uxland(u, d).wait_recv()
-        for j in range(2):
-            ubox[u, :, j] = order(p1t, uinx[u, :, j], (NZ, ZR, C))
+        for d in ZD:
+            uzcopy(u, d).wait_send()
+        ubox[u] = order(p1t, uinx[u], (NZ, ZR, C))
         for d in ZD:
             uzcopy(u, d).start()
         uinz[u, z] = ubox[u, z]
@@ -522,27 +516,34 @@
     def unit_back_z(u):
         for d in ZD:
             uzland(u, d).wait_recv()
-        v, h = u // 2, 1 - u % 2
-        for j in range(2):
-            o = 2 * h + j
-            b = (t + o) % NT
-            got = uinz[u, :, j].reshape(BOTH, C)
-            raw[v, o, rlo] = dot(pltx[b], got).astype(BF16)
-            raw[v, o, rhi] = dot(pltc[b], got).astype(BF16)
-
-        @pl.when(h == 1)
+        v, r = u // NT, u % NT
+
+        @pl.when(r == 0)
+        def _():
+            for i in range(4):
+                rcopy(v, i).wait_send()
+
+        o = gray(3 - r)
+        got = uinz[u].reshape(BOTH, C)
+        raw[v, o, rlo] = dot(pltx[o], got).astype(BF16)
+        raw[v, o, rhi] = dot(pltc[o], got).astype(BF16)
+
+        @pl.when(r == 0)
         def _():
             uacopy(v, 0).start()
             uacopy(v, 1).start()
 
-        @pl.when(h == 0)
+        @pl.when(r == 1)
+        def _():
+            uacopy(v, 1).wait_recv()
+            raw[v, 3, rhi] = (raw[v, 3, rhi].astype(F32) + ua[v, 1].astype(F32)).astype(BF16)
+            ubcopy(v, 1).start()
+
+        @pl.when(r == 2)
         def _():
             uacopy(v, 0).wait_recv()
             raw[v, 1, rlo] = (raw[v, 1, rlo].astype(F32) + ua[v, 0].astype(F32)).astype(BF16)
             ubcopy(v, 0).start()
-            uacopy(v, 1).wait_recv()
-            raw[v, 3, rhi] = (raw[v, 3, rhi].astype(F32) + ua[v, 1].astype(F32)).astype(BF16)
-            ubcopy(v, 1).start()
 
     def unit_sum(v):
         ubcopy(v, 0).wait_recv()
@@ -575,7 +576,7 @@
             for copy in grads_out(s, n):
                 copy.start()
 
-    def vector_0():
+    def vector_0(_):
         @pl.loop(0, NC)
         def _(s):
             three = dot(slope3[...], rows_of(s), TND)
@@ -584,73 +585,27 @@
         for d in YD:
             vycopy(d).start()
 
-    def vector_1():
+    def vector_1(_):
         for d in YD:
             vyland(d).wait_recv()
         vx[q] = (vy[0] + vy[1]) + (vy[2] + vy[3])
         for d in XD:
             vxcopy(d).start()
 
-    def vector_2():
+    def vector_2(_):
         for d in XD:
             vxland(d).wait_recv()
         for d in ZD:
             vzcopy(d).start()
         vz[z] = vx[...]
 
-    @pl.loop(0, 10)
-    def _(j):
-        @pl.when(j < NN)
-        def _():
-            back_far(j)
-
-        @pl.when((j >= 1) & (j < NN + 1))
-        def _():
-            back_near(j - 1)
-
-        @pl.when(j < NU)
-        def _():
-            unit_back(j)
-
-        @pl.when(j == 3)
-        def _():
-            vector_0()
-
-        @pl.when(j == 5)
-        def _():
-            vector_1()
-
-        @pl.when(j == 7)
-        def _():
-            vector_2()
-
-        @pl.when((j >= 3) & (j < NU + 3))
-        def _():
-            unit_back_x(j - 3)
-
-        @pl.when((j >= 4) & (j < NU + 4))
-        def _():
-            unit_back_z(j - 4)
-
-        @pl.when((j >= 4) & (j < NC + 4))
-        def _():
-            grads(j - 4)
-
-        @pl.when((j >= 3) & (j < NN + 3))
-        def _():
-            back_own(j - 3)
-
-        @pl.when((j >= 4) & (j < NN + 4))
-        def _():
-            back_x(j - 4)
-
-        @pl.when((j >= 5) & (j < NN + 5))
-        def _():
-            back_z(j - 5)
-
-        @pl.when(j >= 8)
-        def _():
-            unit_sum(j - 8)
+    @pl.loop(0, BACK_STEPS)
+    def _(i):
+        for task in (
+            back_far, unit_back, vector_0, back_near, unit_back_x, unit_back_z, grads, back_own,
+            vector_1, vector_2, back_x, unit_sum, back_z,
+        ):
+            at(i, BACK[task.__name__], task)
 
     for d in ZD:
         vzland(d).wait_recv()
@@ -665,6 +620,8 @@
 
     @pl.loop(0, NN)
     def _(n):
+        for i in range(4):
+            ycopy(n, i).wait_send()
         for i in range(2):
             acopy(n, i).wait_send()
             bcopy(n, i).wait_send()
@@ -705,10 +662,10 @@
         V((NN, NZ, ZR, C), BF16),
         V((NN, NQ, XR, C), BF16),
         V((NN, NQ, XR, C), BF16),
-        V((NU, NZ, 2, ZR, C), BF16),
-        V((NU, NZ, 2, ZR, C), BF16),
-        V((NU, NQ, 2, XR, C), BF16),
-        V((NU, NQ, 2, XR, C), BF16),
+        V((NU, NZ, ZR, C), BF16),
+        V((NU, NZ, ZR, C), BF16),
+        V((NU, NQ, XR, C), BF16),
+        V((NU, NQ, XR, C), BF16),
         V((NS, NT, 2 * ROWS, C), BF16),
         V((NC, NT, BOTH, C), BF16),
         V((NC, C, H), BF16),

time: 193 us -> 174 us (0.902)
  Pallas kernels: 177 us -> 159 us
    pallas_call x1, Pallas kernels: 177 us -> 159 us  [per_device(): pl.pallas_call(kernel, out_shape=(S((ROWS, width), BF16), S((ROWS, width)...]
where the time goes in v4:
time: 174 us
  Pallas kernels  159 us (91%)
  local copies, waits for them, and re-layouts  13.7 us (8%)
    pallas_call x1, Pallas kernels, per_device(): pl.pallas_call(kernel, out_shape=(S((ROWS, width), BF16), S((ROWS, width)...  159 us
    unnamed x9, local copies, waits for them, and re-layouts  13.7 us

profile of v4, /device:TPU:1, one launch (start us, length us, event | category | flops | bytes accessed | tf_op | source)
XLA Modules:
  0.0 173.9 jit_solution(3639504229916181222)
XLA Ops:
  1.3 158.9 %shard_map.110 = (bf16[128,2560]{1,0:T(8,128)(2,1)}, bf16[128,2560]{1,0:T(8,128)(2,1)}, bf16[1,2560,1024]{2,1,0:T(8,128)(2,1)}, bf16[1,1024,2560]{2,1,0:T(8,128)(2,1)}, f32[32,1,2560]{2,1,0:T(1,128)}) custom-call(s32[1,128]{1,0:T(1,128)} %bitcast.11, s32[1]{0:T(128)S(6)} %copy.19.live_ref, bf16[32,2560]{1,0:T(8,128)(2,1)} %bitcast.10, ...), custom_call_target="tpu_custom_call" | custom-call | tf_op jit(solution)/shard_map/pallas_call | solution.py:712
  160.2 1.7 copy.14
  161.9 2.0 %copy.20 = bf16[128,2560]{1,0:T(8,128)(2,1)} copy(bf16[128,2560]{1,0:T(8,128)(2,1)} %get-tuple-element.20) | data formatting | bytes 1310720
  163.9 0.0 slice-start
  163.9 2.1 %copy.21 = bf16[128,2560]{1,0:T(8,128)(2,1)} copy(bf16[128,2560]{1,0:T(8,128)(2,1)} %get-tuple-element.21) | data formatting | bytes 1310720
  166.0 0.0 slice-start.1
  166.0 5.5 %copy.22 = bf16[1,2560,1024]{2,1,0:T(8,128)(2,1)} copy(bf16[1,2560,1024]{2,1,0:T(8,128)(2,1)} %get-tuple-element.22) | data formatting | bytes 10485760
  171.5 0.0 slice-done
  171.5 0.0 slice-done.1
  171.5 2.4 %copy.23 = bf16[1,1024,2560]{2,1,0:T(8,128)(2,1)} copy(bf16[1,1024,2560]{2,1,0:T(8,128)(2,1)S(1)} %bitcast.8) | data formatting | bytes 10485760
  (1 shorter events, 0.0 us)
Async XLA Ops:
  163.9 7.6 %slice-start = ((s8[5242880]{0:T(1024)(128)(4,1)}), s8[4194304]{0:T(1024)(128)(4,1)S(1)}, s32[]{:S(2)}) async-start(s8[5242880]{0:T(1024)(128)(4,1)} %bitcast.7), calls=%async_computation | async-start | bytes 8388608
  166.0 5.5 %slice-start.1 = ((s8[5242880]{0:T(1024)(128)(4,1)}), s8[1048576]{0:T(1024)(128)(4,1)S(1)}, s32[]{:S(2)}) async-start(s8[5242880]{0:T(1024)(128)(4,1)} %bitcast.7), calls=%async_computation.1 | async-start | bytes 2097152

commit v5 on v4

--- a/solution.py
+++ b/solution.py
@@ -21,35 +21,36 @@
 N = 256
 
 
-OUT_STEPS = 22
+OUT_STEPS = 28
 OUT = dict(
-    out_z=(1, 3, 4,),
-    raw_on=(1, 3,),
-    unit_box=(0, 1, 2, 4, 5, 6, 7, 8,),
-    out_x=(3, 7, 9,),
-    unit_z=(8, 9, 10, 11, 12, 13, 14, 15,),
-    unit_x=(9, 10, 11, 12, 13, 14, 16, 19,),
-    release=(19,),
-    out_y=(9, 11, 13,),
-    near=(9, 10, 11, 13, 14,),
-    away=(16, 17, 18, 19, 20,),
-    middle=(14, 15, 20, 21,),
+    out_z=(2, 4, 5,),
+    raw_on=(1, 4,),
+    unit_box=(0, 2, 3, 5, 6, 7, 8, 9,),
+    out_x=(4, 8, 10,),
+    unit_z=(9, 10, 11, 13, 15, 17, 18, 20,),
+    unit_x=(11, 12, 14, 16, 18, 19, 21, 25,),
+    release=(25,),
+    out_y=(10, 13, 17,),
+    near=(10, 14, 15, 17, 21,),
+    away=(18, 19, 20, 26, 27,),
+    middle=(21, 22, 25, 27,),
+    early=(22, 23, 24,),
 )
-BACK_STEPS = 28
+BACK_STEPS = 25
 BACK = dict(
-    back_far=(0, 1, 2,),
-    unit_back=(2, 3, 4, 5, 6, 7, 8, 9,),
-    vector_0=(9,),
-    back_near=(9, 10, 11,),
-    unit_back_x=(8, 9, 11, 12, 13, 15, 16, 20,),
-    unit_back_z=(10, 16, 17, 18, 19, 23, 24, 25,),
-    grads=(11, 12, 13, 14, 15,),
-    back_own=(12, 15, 21,),
+    unit_back=(0, 1, 2, 3, 4, 5, 6, 7,),
+    back_far=(7, 8, 9,),
+    vector_0=(10,),
+    grads=(10, 11, 12, 13, 16,),
     vector_1=(12,),
-    vector_2=(15,),
-    back_x=(20, 21, 22,),
-    unit_sum=(21, 27,),
-    back_z=(21, 25, 26,),
+    unit_back_x=(6, 9, 10, 11, 12, 13, 16, 18,),
+    unit_back_z=(10, 13, 14, 15, 16, 20, 21, 22,),
+    back_near=(10, 11, 12,),
+    back_own=(16, 17, 18,),
+    vector_2=(16,),
+    back_x=(18, 19, 22,),
+    unit_sum=(19, 24,),
+    back_z=(19, 22, 23,),
 )
 
 
@@ -65,8 +66,8 @@
     return lax.broadcasted_iota(I32, shape, axis).astype(F32)
 
 
-def gray(r):
-    return r + r // 2 - 2 * (r // 3)
+def turn(r):
+    return r + 1 - 3 * (r // 2) + 2 * (r // 3)
 
 
 def at(i, steps, task):
@@ -180,31 +181,32 @@
 
     def ycopy(n, i):
         b = yb.at[normal(n)]
-        src = (b.at[0], b.at[0], b.at[3, lo], b.at[1, hi])[i]
-        dst = (b.at[3], b.at[1], b.at[2, lo], b.at[2, hi])[i]
+        src = (b.at[1], b.at[1], b.at[0, lo], b.at[2, hi])[i]
+        dst = (b.at[0], b.at[2], b.at[3, lo], b.at[3, hi])[i]
         return remote(src, dst, ys.at[n, i], yr.at[n, i], ypeer(SIDE[i]))
 
     def rcopy(v, i):
         b = raw.at[v]
-        src = (b.at[0], b.at[0], b.at[3, rlo], b.at[1, rhi])[i]
-        dst = (b.at[3], b.at[1], b.at[2, rlo], b.at[2, rhi])[i]
+        src = (b.at[1], b.at[1], b.at[0, rlo], b.at[2, rhi])[i]
+        dst = (b.at[0], b.at[2], b.at[3, rlo], b.at[3, rhi])[i]
         return remote(src, dst, rs.at[v, i], rr.at[v, i], ypeer(SIDE[i]))
 
     def acopy(n, i):
         return remote(sa.at[n, i], ra.at[n, i], as_.at[n, i], ar.at[n, i], ypeer(SIDE[i]))
 
     def bcopy(n, i):
-        return remote(sb.at[n, i], rb.at[n, i], bs.at[n, i], br.at[n, i], ypeer(SIDE[i]))
+        k, half = i % 2, (lo, hi, hi, lo)[i]
+        return remote(sb.at[n, k, half], rb.at[n, k, half], bs.at[n, i], br.at[n, i], ypeer(SIDE[i]))
 
     def uacopy(v, i):
-        src = raw.at[v, 2, (rlo, rhi)[i]]
+        src = raw.at[v, 3, (rlo, rhi)[i]]
         return remote(src, ua.at[v, i], uas.at[v, i], uar.at[v, i], ypeer(SIDE[i]))
 
     def ubcopy(v, i):
-        return remote(raw.at[v, SIDE[i]], ub.at[v, i], ubs.at[v, i], ubr.at[v, i], ypeer(SIDE[i]))
+        return remote(raw.at[v, (2, 0)[i]], ub.at[v, i], ubs.at[v, i], ubr.at[v, i], ypeer(SIDE[i]))
 
     def vtcopy(d):
-        return remote(vt.at[0], vt.at[NT - d], vts.at[d], vtr.at[d], ypeer(d))
+        return remote(vt.at[1], vt.at[(1, 0, 3, 2)[d]], vts.at[d], vtr.at[d], ypeer(d))
 
     def vycopy(d):
         return remote(vy.at[t], vy.at[t], vys.at[d], vyr.at[d], ypeer(d))
@@ -259,7 +261,7 @@
     logits = dot(tok_ref[...], router_ref[...], NTD)
     gate = jax.nn.sigmoid(jnp.sum(jnp.where(chosen, logits, 0.0), axis=1, keepdims=True))
     gate_s[...] = jnp.broadcast_to(gate, (ROWS, 128))
-    raw[0, 0] = both_of(special(0))
+    raw[0, 1] = both_of(special(0))
     pl.semaphore_wait(barrier, NZ + NQ + NT - 3)
     rcopy(0, 0).start()
     rcopy(0, 1).start()
@@ -269,17 +271,17 @@
     rank = jnp.sum(jnp.where(chosen, counts, 0.0), axis=1, keepdims=True)
     live = lax.broadcasted_iota(I32, (ROWS, 1), 0) < live_ref[0]
     target = jnp.where(live, ids * (2.0 * MOST) + rank, -1000.0)
-    vt[0] = jnp.sum(jnp.where(diag, target, 0.0), axis=0, keepdims=True)
-    raw[1, 0] = both_of(special(1))
+    vt[1] = jnp.sum(jnp.where(diag, target, 0.0), axis=0, keepdims=True)
+    raw[1, 1] = both_of(special(1))
     for d in YD:
         vtcopy(d).start()
     rcopy(1, 0).start()
     rcopy(1, 1).start()
-    place(0)
+    place(1)
 
     @pl.loop(0, NN)
     def _(n):
-        box[n] = dot(plc[0], both_of(normal(n))).astype(BF16).reshape(NZ, ZR, C)
+        box[n] = dot(plc[1], both_of(normal(n))).astype(BF16).reshape(NZ, ZR, C)
         for d in ZD:
             zcopy(n, d).start()
         inz[n, z] = box[n, z]
@@ -292,7 +294,7 @@
     p2t[...] = onehot(source_2(line) == down)
     for d in YD:
         vtcopy(d).wait_recv()
-        place(NT - d)
+        place((1, 0, 3, 2)[d])
 
     hid[...] = jnp.zeros_like(hid)
     dh[...] = jnp.zeros_like(dh)
@@ -323,7 +325,7 @@
     def out_x(n):
         for d in XD:
             xland(n, d).wait_recv()
-        yb[normal(n), 0] = order(p2, inx[n], (BOTH, C))
+        yb[normal(n), 1] = order(p2, inx[n], (BOTH, C))
         ycopy(n, 0).start()
         ycopy(n, 1).start()
 
@@ -347,7 +349,7 @@
             rcopy(v, 2).wait_recv()
             rcopy(v, 3).wait_recv()
 
-        o = gray(r)
+        o = turn(r)
         ubox[u] = dot(plc[o], raw[v, o]).astype(BF16).reshape(NZ, ZR, C)
         for d in ZD:
             uzcopy(u, d).start()
@@ -364,19 +366,18 @@
     def unit_x(u):
         for d in XD:
             uxland(u, d).wait_recv()
-        yb[special(u // NT), gray(u % NT)] = order(p2, uinx[u], (BOTH, C))
+        yb[special(u // NT), turn(u % NT)] = order(p2, uinx[u], (BOTH, C))
 
     def release(_):
         for peers, ds in ((zpeer, ZD), (xpeer, XD)):
             for d in ds:
                 pl.semaphore_signal(free, inc=1, device_id=peers(d), device_id_type=MESH)
 
-    HALF = 2 * SLOTS
-
-    def work(s, h):
-        r = pl.ds(h * HALF, HALF)
-        rows = yb[s, 2 * h : 2 * h + 2, :SLOTS, :].reshape(HALF, C)
-        cots = yb[s, 2 * h : 2 * h + 2, SLOTS:, :].reshape(HALF, C)
+    def work(s, first, last):
+        size = (last - first) * SLOTS
+        r = pl.ds(first * SLOTS, size)
+        rows = yb[s, first:last, :SLOTS, :].reshape(size, C)
+        cots = yb[s, first:last, SLOTS:, :].reshape(size, C)
         lg[r, :] += dot(rows, router_ref[:, piece(s)], NTD)
 
         @pl.loop(0, H // N)
@@ -388,7 +389,7 @@
     def near(s):
         for copy in weights(s):
             copy.wait()
-        work(s, 0)
+        work(s, 0, 3)
 
     def away(s):
         for n in range(NN):
@@ -398,11 +399,13 @@
                 ycopy(n, 2).wait_recv()
                 ycopy(n, 3).wait_recv()
 
-        work(s, 1)
+        work(s, 3, 4)
 
     BR = 32
 
-    def middle(o):
+    def middle(k):
+        o = 2 * k - 3 * (k // 2)
+
         @pl.loop(0, SLOTS // BR)
         def _(b):
             silu_rows(pl.ds(pl.multiple_of(o * SLOTS + b * BR, BR), BR))
@@ -426,40 +429,48 @@
             k == 0.0, s1, jnp.where(k == 1.0, s2, jnp.where(k == 2.0, s3, 0.0))
         ).astype(BF16)
 
+    def value_of(s, o):
+        r = pl.ds(pl.multiple_of(o * SLOTS, SLOTS), SLOTS)
+        return dot(act[r, :], wd[s])
+
+    def grad_of(s, o):
+        r = pl.ds(pl.multiple_of(o * SLOTS, SLOTS), SLOTS)
+        return dot(hc[r, :], wu[s], NTD) + slope_s[r, :1] * rrow[s, :1, :]
+
+    def early(n):
+        s = normal(n)
+        sb[n, 0, hi] = grad_of(s, 2).astype(BF16)
+        bcopy(n, 2).start()
+        sb[n, 1, lo] = value_of(s, 0).astype(BF16)
+        bcopy(n, 3).start()
+
     @pl.loop(0, OUT_STEPS)
     def _(i):
-        for task in (out_z, raw_on, unit_box, out_x, unit_z, unit_x, release, out_y, near, away, middle):
+        for task in (out_z, raw_on, unit_box, out_x, unit_z, unit_x, release, out_y, near, away, middle, early):
             at(i, OUT[task.__name__], task)
 
-    def partial(s, b):
-        r = pl.ds(pl.multiple_of(b * SLOTS, SLOTS), SLOTS)
-        value = dot(act[r, :], wd[s])
-        grad = dot(hc[r, :], wu[s], NTD) + slope_s[r, :1] * rrow[s, :1, :]
-        return value, grad
-
     def back_far(n):
-        value, grad = partial(normal(n), 2)
-        sa[n, 0] = value.astype(BF16)
-        sa[n, 1] = grad.astype(BF16)
+        s = normal(n)
+        sa[n, 0] = value_of(s, 3).astype(BF16)
         acopy(n, 0).start()
+        sa[n, 1] = grad_of(s, 3).astype(BF16)
         acopy(n, 1).start()
 
     def back_near(n):
-        value, grad = partial(normal(n), 1)
+        s = normal(n)
+        value = value_of(s, 2)
         acopy(n, 0).wait_recv()
         sb[n, 0, lo] = (value + ra[n, 0].astype(F32)).astype(BF16)
-        sb[n, 0, hi] = grad.astype(BF16)
         bcopy(n, 0).start()
-        value, grad = partial(normal(n), 3)
+        grad = grad_of(s, 0)
         acopy(n, 1).wait_recv()
-        sb[n, 1, lo] = value.astype(BF16)
         sb[n, 1, hi] = (grad + ra[n, 1].astype(F32)).astype(BF16)
         bcopy(n, 1).start()
 
     def back_own(n):
-        value, grad = partial(normal(n), 0)
-        bcopy(n, 0).wait_recv()
-        bcopy(n, 1).wait_recv()
+        value, grad = value_of(normal(n), 1), grad_of(normal(n), 1)
+        for i in range(4):
+            bcopy(n, i).wait_recv()
         value = value + rb[n, 0, :SLOTS, :].astype(F32) + rb[n, 1, :SLOTS, :].astype(F32)
         grad = grad + rb[n, 0, SLOTS:, :].astype(F32) + rb[n, 1, SLOTS:, :].astype(F32)
         both = jnp.concatenate([value, grad], axis=0).astype(BF16)
@@ -485,11 +496,12 @@
             zland(n, d).wait_recv()
         got = inz[n].reshape(BOTH, C)
         cols = piece(normal(n))
-        mixed_ref[:, cols] = (gate_s[:, :1] * dot(pltx[0], got)).astype(BF16)
-        tgrad_ref[:, cols] = dot(pltc[0], got).astype(BF16)
+        mixed_ref[:, cols] = (gate_s[:, :1] * dot(pltx[1], got)).astype(BF16)
+        tgrad_ref[:, cols] = dot(pltc[1], got).astype(BF16)
 
     def unit_back(u):
-        value, grad = partial(special(u // NT), gray(3 - u % NT))
+        s, o = special(u // NT), turn(3 - u % NT)
+        value, grad = value_of(s, o), grad_of(s, o)
         both = jnp.concatenate([value, grad], axis=0).astype(BF16)
         for d in XD:
             uxcopy(u, d).wait_send()
@@ -523,7 +535,7 @@
             for i in range(4):
                 rcopy(v, i).wait_send()
 
-        o = gray(3 - r)
+        o = turn(3 - r)
         got = uinz[u].reshape(BOTH, C)
         raw[v, o, rlo] = dot(pltx[o], got).astype(BF16)
         raw[v, o, rhi] = dot(pltc[o], got).astype(BF16)
@@ -536,19 +548,19 @@
         @pl.when(r == 1)
         def _():
             uacopy(v, 1).wait_recv()
-            raw[v, 3, rhi] = (raw[v, 3, rhi].astype(F32) + ua[v, 1].astype(F32)).astype(BF16)
+            raw[v, 0, rhi] = (raw[v, 0, rhi].astype(F32) + ua[v, 1].astype(F32)).astype(BF16)
             ubcopy(v, 1).start()
 
         @pl.when(r == 2)
         def _():
             uacopy(v, 0).wait_recv()
-            raw[v, 1, rlo] = (raw[v, 1, rlo].astype(F32) + ua[v, 0].astype(F32)).astype(BF16)
+            raw[v, 2, rlo] = (raw[v, 2, rlo].astype(F32) + ua[v, 0].astype(F32)).astype(BF16)
             ubcopy(v, 0).start()
 
     def unit_sum(v):
         ubcopy(v, 0).wait_recv()
         ubcopy(v, 1).wait_recv()
-        got = raw[v, 0].astype(F32) + ub[v, 0].astype(F32) + ub[v, 1].astype(F32)
+        got = raw[v, 1].astype(F32) + ub[v, 0].astype(F32) + ub[v, 1].astype(F32)
         cols = piece(special(v))
         value = got[:ROWS].astype(BF16).astype(F32)
         mixed_ref[:, cols] = (gate_s[:, :1] * value).astype(BF16)
@@ -602,14 +614,14 @@
     @pl.loop(0, BACK_STEPS)
     def _(i):
         for task in (
-            back_far, unit_back, vector_0, back_near, unit_back_x, unit_back_z, grads, back_own,
-            vector_1, vector_2, back_x, unit_sum, back_z,
+            unit_back, back_far, vector_0, grads, vector_1, unit_back_x, unit_back_z, back_near, back_own,
+            vector_2, back_x, unit_sum, back_z,
         ):
             at(i, BACK[task.__name__], task)
 
     for d in ZD:
         vzland(d).wait_recv()
-    rgrad_ref[...] = vz[...].reshape(EXPERTS, 1, C * NC)
+    rgrad_ref[...] = vz[...].reshape(EXPERTS, C * NC)
     for d in YD:
         vtcopy(d).wait_send()
         vycopy(d).wait_send()
@@ -622,9 +634,9 @@
     def _(n):
         for i in range(4):
             ycopy(n, i).wait_send()
+            bcopy(n, i).wait_send()
         for i in range(2):
             acopy(n, i).wait_send()
-            bcopy(n, i).wait_send()
         for d in XD:
             xcopy(n, d).wait_send()
         for d in ZD:
@@ -646,6 +658,45 @@
     for n in range(2):
         for copy in grads_out(NC - 1, n):
             copy.wait()
+
+
+def hand_over(arrays):
+    cuts = []
+    for k, a in enumerate(arrays):
+        axis = len(a.shape) - 2
+        parts = 4 if a.size > 1 << 20 else 1
+        size = a.shape[axis] // parts
+        cuts += [(k, (slice(None),) * axis + (pl.ds(p * size, size),)) for p in range(parts)]
+
+    def body(*refs):
+        n = len(arrays)
+        ins, outs, bufs, sems = refs[:n], refs[n : 2 * n], refs[2 * n : 3 * n], refs[3 * n]
+        reads = [
+            pltpu.make_async_copy(ins[k].at[c], bufs[k].at[c], sems.at[0, i])
+            for i, (k, c) in enumerate(cuts)
+        ]
+        writes = [
+            pltpu.make_async_copy(bufs[k].at[c], outs[k].at[c], sems.at[1, i])
+            for i, (k, c) in enumerate(cuts)
+        ]
+        for copy in reads:
+            copy.start()
+        for read, write in zip(reads, writes):
+            read.wait()
+            write.start()
+        for copy in writes:
+            copy.wait()
+
+    hbm = pl.BlockSpec(memory_space=pl.ANY)
+    return pl.pallas_call(
+        body,
+        out_shape=tuple(jax.ShapeDtypeStruct(a.shape, a.dtype) for a in arrays),
+        in_specs=[hbm] * len(arrays),
+        out_specs=(hbm,) * len(arrays),
+        scratch_shapes=[pltpu.VMEM(a.shape, a.dtype) for a in arrays]
+        + [pltpu.SemaphoreType.DMA((2, len(cuts)))],
+        compiler_params=pltpu.CompilerParams(vmem_limit_bytes=60 << 20),
+    )(*arrays)
 
 
 def per_device(tokens, expert_ids, live_counts, router, up_weight, down_weight, out_grad):
@@ -700,7 +751,7 @@
         V((NZ, NQ, 1, width), F32),
         DMA((2, NC)),
         DMA((NN, NZ)), DMA((NN, NZ)), DMA((NN, NQ)), DMA((NN, NQ)), DMA((NN, 4)), DMA((NN, 4)),
-        DMA((NN, 2)), DMA((NN, 2)), DMA((NN, 2)), DMA((NN, 2)),
+        DMA((NN, 2)), DMA((NN, 2)), DMA((NN, 4)), DMA((NN, 4)),
         DMA((NU, NZ)), DMA((NU, NZ)), DMA((NU, NQ)), DMA((NU, NQ)), DMA((NS, 4)), DMA((NS, 4)),
         DMA((NS, 2)), DMA((NS, 2)), DMA((NS, 2)), DMA((NS, 2)),
         DMA((2, 2)),
@@ -709,14 +760,14 @@
         pltpu.SemaphoreType.REGULAR,
     ]
     S = jax.ShapeDtypeStruct
-    mixed, tgrad, upg, downg, rgrad = pl.pallas_call(
+    results = pl.pallas_call(
         kernel,
         out_shape=(
             S((ROWS, width), BF16),
             S((ROWS, width), BF16),
             S((1, width, H), BF16),
             S((1, H, width), BF16),
-            S((EXPERTS, 1, width), F32),
+            S((EXPERTS, width), F32),
         ),
         in_specs=[vmem, smem, vmem, vmem, vmem, hbm, hbm],
         out_specs=(vmem, vmem, hbm, hbm, vmem),
@@ -727,7 +778,8 @@
     )(
         expert_ids.reshape(1, ROWS), live_counts, router.T, tokens, out_grad, up_weight, down_weight
     )
-    return (mixed, tgrad, upg, downg, rgrad.reshape(EXPERTS, width).T)
+    mixed, tgrad, upg, downg, rgrad = hand_over(results)
+    return (mixed, tgrad, upg, downg, rgrad.T)
 
 
 def solution(mesh):

time: 174 us -> 164 us (0.943)
  local copies, waits for them, and re-layouts: 13.7 us -> 0 us
  Pallas kernels: 159 us -> 163 us
    unnamed x9 -> x0, local copies, waits for them, and re-layouts: 13.7 us -> none
    pallas_call x0 -> x1, Pallas kernels: none -> 8.89 us  [hand_over(): pl.pallas_call(body, out_shape=tuple((jax.ShapeDtypeStruct(a.shape, a.dty...]
    pallas_call x1, Pallas kernels: 159 us -> 154 us  [per_device(): pl.pallas_call(kernel, out_shape=(S((ROWS, width), BF16), S((ROWS, width)...]
where the time goes in v5:
time: 164 us
  Pallas kernels  163 us (99%)
    pallas_call x1, Pallas kernels, per_device(): pl.pallas_call(kernel, out_shape=(S((ROWS, width), BF16), S((ROWS, width)...  154 us
    pallas_call x1, Pallas kernels, hand_over(): pl.pallas_call(body, out_shape=tuple((jax.ShapeDtypeStruct(a.shape, a.dty...  8.89 us

profile of v5, /device:TPU:1, one launch (start us, length us, event | category | flops | bytes accessed | tf_op | source)
XLA Modules:
  0.0 163.8 jit_solution(13921927351122172636)
XLA Ops:
  1.3 153.6 %shard_map.110 = (bf16[128,2560]{1,0:T(8,128)(2,1)}, bf16[128,2560]{1,0:T(8,128)(2,1)}, bf16[1,2560,1024]{2,1,0:T(8,128)(2,1)}, bf16[1,1024,2560]{2,1,0:T(8,128)(2,1)}, f32[32,2560]{1,0:T(8,128)}) custom-call(s32[1,128]{1,0:T(1,128)} %bitcast.4, s32[1]{0:T(128)S(6)} %copy.12.live_ref, bf16[32,2560]{1,0:T(8,128)(2,1)} %bitcast.3, bf16[128,2560]{1,0:T(8,128)(2,1)} %tok_ref.1, ...), custom_call_target="tpu_custom_call" | custom-call | tf_op jit(solution)/shard_map/pallas_call | solution.py:763
  154.9 8.9 %shard_map.111 = (bf16[128,2560]{1,0:T(8,128)(2,1)}, bf16[128,2560]{1,0:T(8,128)(2,1)}, bf16[1,2560,1024]{2,1,0:T(8,128)(2,1)}, bf16[1,1024,2560]{2,1,0:T(8,128)(2,1)}, f32[32,2560]{1,0:T(8,128)}) custom-call(bf16[128,2560]{1,0:T(8,128)(2,1)} %get-tuple-element.15.refs_0_, bf16[128,2560]{1,0:T(8,128)(2,1)} %get-tuple-element.16.refs_1_, ...), custom_call_target="tpu_custom_call" | custom-call | tf_op jit(solution)/shard_map/pallas_call | solution.py:691

commit v6 on v5

--- a/solution.py
+++ b/solution.py
@@ -23,34 +23,34 @@
 
 OUT_STEPS = 28
 OUT = dict(
-    out_z=(2, 4, 5,),
     raw_on=(1, 4,),
-    unit_box=(0, 2, 3, 5, 6, 7, 8, 9,),
-    out_x=(4, 8, 10,),
-    unit_z=(9, 10, 11, 13, 15, 17, 18, 20,),
-    unit_x=(11, 12, 14, 16, 18, 19, 21, 25,),
-    release=(25,),
+    early=(23, 24, 25,),
+    out_x=(4, 8, 9,),
+    release=(26,),
+    out_z=(1, 3, 4,),
     out_y=(10, 13, 17,),
-    near=(10, 14, 15, 17, 21,),
+    unit_box=(0, 1, 2, 4, 5, 6, 7, 8,),
+    near=(10, 15, 16, 17, 21,),
+    unit_z=(8, 9, 10, 12, 14, 16, 17, 19,),
     away=(18, 19, 20, 26, 27,),
     middle=(21, 22, 25, 27,),
-    early=(22, 23, 24,),
+    unit_x=(10, 11, 13, 16, 17, 18, 20, 25,),
 )
-BACK_STEPS = 25
+BACK_STEPS = 24
 BACK = dict(
     unit_back=(0, 1, 2, 3, 4, 5, 6, 7,),
+    back_own=(16, 17, 18,),
+    back_x=(18, 19, 22,),
     back_far=(7, 8, 9,),
-    vector_0=(10,),
-    grads=(10, 11, 12, 13, 16,),
-    vector_1=(12,),
-    unit_back_x=(6, 9, 10, 11, 12, 13, 16, 18,),
-    unit_back_z=(10, 13, 14, 15, 16, 20, 21, 22,),
-    back_near=(10, 11, 12,),
-    back_own=(16, 17, 18,),
-    vector_2=(16,),
-    back_x=(18, 19, 22,),
-    unit_sum=(19, 24,),
-    back_z=(19, 22, 23,),
+    grads=(9, 10, 11, 12, 13,),
+    vector_1=(16,),
+    vector_2=(19,),
+    vector_0=(13,),
+    unit_back_x=(6, 9, 11, 12, 13, 15, 16, 17,),
+    unit_sum=(19, 23,),
+    back_near=(11, 12, 13,),
+    unit_back_z=(10, 13, 14, 15, 16, 19, 20, 21,),
+    back_z=(21, 22, 23,),
 )
 
 
@@ -71,13 +71,15 @@
 
 
 def at(i, steps, task):
-    here, k = i == steps[0], 0
+    here = i == steps[0]
     for step in steps[1:]:
         here = here | (i == step)
-        k = k + (i + 64 - step) // 64
 
     @pl.when(here)
     def _():
+        k = 0
+        for step in steps[1:]:
+            k = k + (i + 64 - step) // 64
         task(k)
 
 
@@ -154,28 +156,32 @@
         )
 
     def zcopy(n, d):
-        return remote(box.at[n, (z + d) % NZ], inz.at[n, z], zs.at[n, d], zr.at[n, d], zpeer(d))
-
-    def zland(n, d):
-        return remote(box.at[n, z], inz.at[n, (z + NZ - d) % NZ], zs.at[n, d], zr.at[n, d], zpeer(d))
+        return remote(box.at[n, (z + d) % NZ], inz.at[n, z], zs.at[n], zr.at[n], zpeer(d))
+
+    def zall(n):
+        some = pl.ds(0, NZ - 1)
+        return remote(box.at[n, some], inz.at[n, some], zs.at[n], zr.at[n], zpeer(1))
 
     def xcopy(n, d):
-        return remote(outx.at[n, (q + d) % NQ], inx.at[n, q], xs.at[n, d], xr.at[n, d], xpeer(d))
-
-    def xland(n, d):
-        return remote(outx.at[n, q], inx.at[n, (q + NQ - d) % NQ], xs.at[n, d], xr.at[n, d], xpeer(d))
+        return remote(outx.at[n, (q + d) % NQ], inx.at[n, q], xs.at[n], xr.at[n], xpeer(d))
+
+    def xall(n):
+        some = pl.ds(0, NQ - 1)
+        return remote(outx.at[n, some], inx.at[n, some], xs.at[n], xr.at[n], xpeer(1))
 
     def uzcopy(u, d):
-        return remote(ubox.at[u, (z + d) % NZ], uinz.at[u, z], uzs.at[u, d], uzr.at[u, d], zpeer(d))
-
-    def uzland(u, d):
-        return remote(ubox.at[u, z], uinz.at[u, (z + NZ - d) % NZ], uzs.at[u, d], uzr.at[u, d], zpeer(d))
+        return remote(ubox.at[u, (z + d) % NZ], uinz.at[u, z], uzs.at[u], uzr.at[u], zpeer(d))
+
+    def uzall(u):
+        some = pl.ds(0, NZ - 1)
+        return remote(ubox.at[u, some], uinz.at[u, some], uzs.at[u], uzr.at[u], zpeer(1))
 
     def uxcopy(u, d):
-        return remote(uoutx.at[u, (q + d) % NQ], uinx.at[u, q], uxs.at[u, d], uxr.at[u, d], xpeer(d))
-
-    def uxland(u, d):
-        return remote(uoutx.at[u, q], uinx.at[u, (q + NQ - d) % NQ], uxs.at[u, d], uxr.at[u, d], xpeer(d))
+        return remote(uoutx.at[u, (q + d) % NQ], uinx.at[u, q], uxs.at[u], uxr.at[u], xpeer(d))
+
+    def uxall(u):
+        some = pl.ds(0, NQ - 1)
+        return remote(uoutx.at[u, some], uinx.at[u, some], uxs.at[u], uxr.at[u], xpeer(1))
 
     SIDE = (1, NT - 1, 1, NT - 1)
 
@@ -315,16 +321,14 @@
         return dot(perm[...], rows.reshape(BOTH, C)).astype(BF16).reshape(shape)
 
     def out_z(n):
-        for d in ZD:
-            zland(n, d).wait_recv()
+        zall(n).wait_recv()
         outx[n] = order(p1, inz[n], (NQ, XR, C))
         for d in XD:
             xcopy(n, d).start()
         inx[n, q] = outx[n, q]
 
     def out_x(n):
-        for d in XD:
-            xland(n, d).wait_recv()
+        xall(n).wait_recv()
         yb[normal(n), 1] = order(p2, inx[n], (BOTH, C))
         ycopy(n, 0).start()
         ycopy(n, 1).start()
@@ -356,16 +360,14 @@
         uinz[u, z] = ubox[u, z]
 
     def unit_z(u):
-        for d in ZD:
-            uzland(u, d).wait_recv()
+        uzall(u).wait_recv()
         uoutx[u] = order(p1, uinz[u], (NQ, XR, C))
         for d in XD:
             uxcopy(u, d).start()
         uinx[u, q] = uoutx[u, q]
 
     def unit_x(u):
-        for d in XD:
-            uxland(u, d).wait_recv()
+        uxall(u).wait_recv()
         yb[special(u // NT), turn(u % NT)] = order(p2, uinx[u], (BOTH, C))
 
     def release(_):
@@ -446,7 +448,9 @@
 
     @pl.loop(0, OUT_STEPS)
     def _(i):
-        for task in (out_z, raw_on, unit_box, out_x, unit_z, unit_x, release, out_y, near, away, middle, early):
+        for task in (
+            raw_on, early, out_x, release, out_z, out_y, unit_box, near, unit_z, away, middle, unit_x,
+        ):
             at(i, OUT[task.__name__], task)
 
     def back_far(n):
@@ -474,26 +478,22 @@
         value = value + rb[n, 0, :SLOTS, :].astype(F32) + rb[n, 1, :SLOTS, :].astype(F32)
         grad = grad + rb[n, 0, SLOTS:, :].astype(F32) + rb[n, 1, SLOTS:, :].astype(F32)
         both = jnp.concatenate([value, grad], axis=0).astype(BF16)
-        for d in XD:
-            xcopy(n, d).wait_send()
+        xall(n).wait_send()
         outx[n] = order(p2t, both, (NQ, XR, C))
         for d in XD:
             xcopy(n, d).start()
         inx[n, q] = outx[n, q]
 
     def back_x(n):
-        for d in XD:
-            xland(n, d).wait_recv()
-        for d in ZD:
-            zcopy(n, d).wait_send()
+        xall(n).wait_recv()
+        zall(n).wait_send()
         box[n] = order(p1t, inx[n], (NZ, ZR, C))
         for d in ZD:
             zcopy(n, d).start()
         inz[n, z] = box[n, z]
 
     def back_z(n):
-        for d in ZD:
-            zland(n, d).wait_recv()
+        zall(n).wait_recv()
         got = inz[n].reshape(BOTH, C)
         cols = piece(normal(n))
         mixed_ref[:, cols] = (gate_s[:, :1] * dot(pltx[1], got)).astype(BF16)
@@ -503,8 +503,7 @@
         s, o = special(u // NT), turn(3 - u % NT)
         value, grad = value_of(s, o), grad_of(s, o)
         both = jnp.concatenate([value, grad], axis=0).astype(BF16)
-        for d in XD:
-            uxcopy(u, d).wait_send()
+        uxall(u).wait_send()
         uoutx[u] = order(p2t, both, (NQ, XR, C))
 
         @pl.when(u == 0)
@@ -516,18 +515,15 @@
         uinx[u, q] = uoutx[u, q]
 
     def unit_back_x(u):
-        for d in XD:
-            uxland(u, d).wait_recv()
-        for d in ZD:
-            uzcopy(u, d).wait_send()
+        uxall(u).wait_recv()
+        uzall(u).wait_send()
         ubox[u] = order(p1t, uinx[u], (NZ, ZR, C))
         for d in ZD:
             uzcopy(u, d).start()
         uinz[u, z] = ubox[u, z]
 
     def unit_back_z(u):
-        for d in ZD:
-            uzland(u, d).wait_recv()
+        uzall(u).wait_recv()
         v, r = u // NT, u % NT
 
         @pl.when(r == 0)
@@ -614,8 +610,7 @@
     @pl.loop(0, BACK_STEPS)
     def _(i):
         for task in (
-            unit_back, back_far, vector_0, grads, vector_1, unit_back_x, unit_back_z, back_near, back_own,
-            vector_2, back_x, unit_sum, back_z,
+            unit_back, back_own, back_x, back_far, grads, vector_1, vector_2, vector_0, unit_back_x, unit_sum, back_near, unit_back_z, back_z,
         ):
             at(i, BACK[task.__name__], task)
 
@@ -637,17 +632,13 @@
             bcopy(n, i).wait_send()
         for i in range(2):
             acopy(n, i).wait_send()
-        for d in XD:
-            xcopy(n, d).wait_send()
-        for d in ZD:
-            zcopy(n, d).wait_send()
+        xall(n).wait_send()
+        zall(n).wait_send()
 
     @pl.loop(0, NU)
     def _(u):
-        for d in XD:
-            uxcopy(u, d).wait_send()
-        for d in ZD:
-            uzcopy(u, d).wait_send()
+        uxall(u).wait_send()
+        uzall(u).wait_send()
 
     @pl.loop(0, NS)
     def _(v):
@@ -750,9 +741,9 @@
         V((NQ, 1, width), F32),
         V((NZ, NQ, 1, width), F32),
         DMA((2, NC)),
-        DMA((NN, NZ)), DMA((NN, NZ)), DMA((NN, NQ)), DMA((NN, NQ)), DMA((NN, 4)), DMA((NN, 4)),
+        DMA((NN,)), DMA((NN,)), DMA((NN,)), DMA((NN,)), DMA((NN, 4)), DMA((NN, 4)),
         DMA((NN, 2)), DMA((NN, 2)), DMA((NN, 4)), DMA((NN, 4)),
-        DMA((NU, NZ)), DMA((NU, NZ)), DMA((NU, NQ)), DMA((NU, NQ)), DMA((NS, 4)), DMA((NS, 4)),
+        DMA((NU,)), DMA((NU,)), DMA((NU,)), DMA((NU,)), DMA((NS, 4)), DMA((NS, 4)),
         DMA((NS, 2)), DMA((NS, 2)), DMA((NS, 2)), DMA((NS, 2)),
         DMA((2, 2)),
         DMA((NT,)), DMA((NT,)), DMA((NT,)), DMA((NT,)),

time: 164 us -> 162 us (0.988)
  Pallas kernels: 163 us -> 161 us
where the time goes in v6:
time: 162 us
  Pallas kernels  161 us (99%)
    pallas_call x1, Pallas kernels, per_device(): pl.pallas_call(kernel, out_shape=(S((ROWS, width), BF16), S((ROWS, width)...  152 us
    pallas_call x1, Pallas kernels, hand_over(): pl.pallas_call(body, out_shape=tuple((jax.ShapeDtypeStruct(a.shape, a.dty...  8.89 us

profile of v6, /device:TPU:1, one launch (start us, length us, event | category | flops | bytes accessed | tf_op | source)
XLA Modules:
  0.0 162.2 jit_solution(13953321577597332312)
XLA Ops:
  1.3 152.0 %shard_map.110 = (bf16[128,2560]{1,0:T(8,128)(2,1)}, bf16[128,2560]{1,0:T(8,128)(2,1)}, bf16[1,2560,1024]{2,1,0:T(8,128)(2,1)}, bf16[1,1024,2560]{2,1,0:T(8,128)(2,1)}, f32[32,2560]{1,0:T(8,128)}) custom-call(s32[1,128]{1,0:T(1,128)} %bitcast.4, s32[1]{0:T(128)S(6)} %copy.12.live_ref, bf16[32,2560]{1,0:T(8,128)(2,1)} %bitcast.3, bf16[128,2560]{1,0:T(8,128)(2,1)} %tok_ref.1, ...), custom_call_target="tpu_custom_call" | custom-call | tf_op jit(solution)/shard_map/pallas_call | solution.py:754
  153.3 8.9 %shard_map.111 = (bf16[128,2560]{1,0:T(8,128)(2,1)}, bf16[128,2560]{1,0:T(8,128)(2,1)}, bf16[1,2560,1024]{2,1,0:T(8,128)(2,1)}, bf16[1,1024,2560]{2,1,0:T(8,128)(2,1)}, f32[32,2560]{1,0:T(8,128)}) custom-call(bf16[128,2560]{1,0:T(8,128)(2,1)} %get-tuple-element.15.refs_0_, bf16[128,2560]{1,0:T(8,128)(2,1)} %get-tuple-element.16.refs_1_, ...), custom_call_target="tpu_custom_call" | custom-call | tf_op jit(solution)/shard_map/pallas_call | solution.py:682

commit v7 on v6

--- a/solution.py
+++ b/solution.py
@@ -21,36 +21,37 @@
 N = 256
 
 
-OUT_STEPS = 28
+OUT_STEPS = 24
 OUT = dict(
-    raw_on=(1, 4,),
-    early=(23, 24, 25,),
-    out_x=(4, 8, 9,),
-    release=(26,),
-    out_z=(1, 3, 4,),
-    out_y=(10, 13, 17,),
-    unit_box=(0, 1, 2, 4, 5, 6, 7, 8,),
-    near=(10, 15, 16, 17, 21,),
-    unit_z=(8, 9, 10, 12, 14, 16, 17, 19,),
-    away=(18, 19, 20, 26, 27,),
-    middle=(21, 22, 25, 27,),
-    unit_x=(10, 11, 13, 16, 17, 18, 20, 25,),
+    out_z=(0, 1, 2,),
+    unit_box=(0, 2, 3, 4, 5, 7, 8, 10,),
+    unit_z=(5, 8, 9, 10, 12, 14, 15, 16,),
+    unit_x=(9, 10, 11, 14, 15, 16, 18, 22,),
+    release=(22,),
+    out_y=(9, 13, 14,),
+    raw_on=(0, 1,),
+    unit_work=(15, 17, 19,),
+    away=(16, 17, 20, 22, 23,),
+    out_x=(1, 5, 6,),
+    near=(9, 12, 13, 14,),
+    early=(20, 21, 23,),
+    middle=(15, 18, 19, 23,),
 )
-BACK_STEPS = 24
+BACK_STEPS = 23
 BACK = dict(
-    unit_back=(0, 1, 2, 3, 4, 5, 6, 7,),
-    back_own=(16, 17, 18,),
-    back_x=(18, 19, 22,),
-    back_far=(7, 8, 9,),
-    grads=(9, 10, 11, 12, 13,),
-    vector_1=(16,),
-    vector_2=(19,),
-    vector_0=(13,),
-    unit_back_x=(6, 9, 11, 12, 13, 15, 16, 17,),
-    unit_sum=(19, 23,),
-    back_near=(11, 12, 13,),
-    unit_back_z=(10, 13, 14, 15, 16, 19, 20, 21,),
-    back_z=(21, 22, 23,),
+    unit_back_x=(4, 6, 7, 9, 10, 11, 13, 15,),
+    unit_back=(0, 1, 2, 3, 4, 5, 6, 9,),
+    back_near=(7, 8, 10,),
+    back_x=(16, 17, 19,),
+    grads=(6, 12, 13, 20, 22,),
+    vector_0=(6,),
+    back_own=(10, 14, 15,),
+    vector_2=(14,),
+    unit_sum=(20, 22,),
+    back_z=(20, 21, 22,),
+    back_far=(1, 2, 4,),
+    unit_back_z=(7, 11, 12, 13, 15, 17, 18, 19,),
+    vector_1=(10,),
 )
 
 
@@ -375,11 +376,11 @@
             for d in ds:
                 pl.semaphore_signal(free, inc=1, device_id=peers(d), device_id_type=MESH)
 
-    def work(s, first, last):
-        size = (last - first) * SLOTS
-        r = pl.ds(first * SLOTS, size)
-        rows = yb[s, first:last, :SLOTS, :].reshape(size, C)
-        cots = yb[s, first:last, SLOTS:, :].reshape(size, C)
+    def work(s, first, count):
+        size = count * SLOTS
+        r = pl.ds(pl.multiple_of(first * SLOTS, SLOTS), size)
+        rows = yb[s, pl.ds(first, count), :SLOTS, :].reshape(size, C)
+        cots = yb[s, pl.ds(first, count), SLOTS:, :].reshape(size, C)
         lg[r, :] += dot(rows, router_ref[:, piece(s)], NTD)
 
         @pl.loop(0, H // N)
@@ -393,6 +394,16 @@
             copy.wait()
         work(s, 0, 3)
 
+    def unit_work(r):
+        s = special(NS - 1)
+
+        @pl.when(r == 0)
+        def _():
+            for copy in weights(s):
+                copy.wait()
+
+        work(s, turn(r), 1)
+
     def away(s):
         for n in range(NN):
 
@@ -401,12 +412,12 @@
                 ycopy(n, 2).wait_recv()
                 ycopy(n, 3).wait_recv()
 
-        work(s, 3, 4)
+        work(s, 3, 1)
 
     BR = 32
 
     def middle(k):
-        o = 2 * k - 3 * (k // 2)
+        o = turn(k)
 
         @pl.loop(0, SLOTS // BR)
         def _(b):
@@ -449,7 +460,7 @@
     @pl.loop(0, OUT_STEPS)
     def _(i):
         for task in (
-            raw_on, early, out_x, release, out_z, out_y, unit_box, near, unit_z, away, middle, unit_x,
+            out_z, unit_box, unit_z, unit_x, release, out_y, raw_on, unit_work, away, out_x, near, early, middle,
         ):
             at(i, OUT[task.__name__], task)
 
@@ -610,7 +621,7 @@
     @pl.loop(0, BACK_STEPS)
     def _(i):
         for task in (
-            unit_back, back_own, back_x, back_far, grads, vector_1, vector_2, vector_0, unit_back_x, unit_sum, back_near, unit_back_z, back_z,
+            unit_back_x, unit_back, back_near, back_x, grads, vector_0, back_own, vector_2, unit_sum, back_z, back_far, unit_back_z, vector_1,
         ):
             at(i, BACK[task.__name__], task)
 

time: 162 us -> 158 us (0.975)
  Pallas kernels: 161 us -> 157 us
    pallas_call x1, Pallas kernels: 152 us -> 148 us  [per_device(): pl.pallas_call(kernel, out_shape=(S((ROWS, width), BF16), S((ROWS, width)...]
where the time goes in v7:
time: 158 us
  Pallas kernels  157 us (99%)
    pallas_call x1, Pallas kernels, per_device(): pl.pallas_call(kernel, out_shape=(S((ROWS, width), BF16), S((ROWS, width)...  148 us
    pallas_call x1, Pallas kernels, hand_over(): pl.pallas_call(body, out_shape=tuple((jax.ShapeDtypeStruct(a.shape, a.dty...  8.89 us

profile of v7, /device:TPU:1, one launch (start us, length us, event | category | flops | bytes accessed | tf_op | source)
XLA Modules:
  0.0 158.1 jit_solution(14046561175878479172)
XLA Ops:
  1.3 147.9 %shard_map.110 = (bf16[128,2560]{1,0:T(8,128)(2,1)}, bf16[128,2560]{1,0:T(8,128)(2,1)}, bf16[1,2560,1024]{2,1,0:T(8,128)(2,1)}, bf16[1,1024,2560]{2,1,0:T(8,128)(2,1)}, f32[32,2560]{1,0:T(8,128)}) custom-call(s32[1,128]{1,0:T(1,128)} %bitcast.4, s32[1]{0:T(128)S(6)} %copy.12.live_ref, bf16[32,2560]{1,0:T(8,128)(2,1)} %bitcast.3, bf16[128,2560]{1,0:T(8,128)(2,1)} %tok_ref.1, ...), custom_call_target="tpu_custom_call" | custom-call | tf_op jit(solution)/shard_map/pallas_call | solution.py:765
  149.2 8.9 %shard_map.111 = (bf16[128,2560]{1,0:T(8,128)(2,1)}, bf16[128,2560]{1,0:T(8,128)(2,1)}, bf16[1,2560,1024]{2,1,0:T(8,128)(2,1)}, bf16[1,1024,2560]{2,1,0:T(8,128)(2,1)}, f32[32,2560]{1,0:T(8,128)}) custom-call(bf16[128,2560]{1,0:T(8,128)(2,1)} %get-tuple-element.15.refs_0_, bf16[128,2560]{1,0:T(8,128)(2,1)} %get-tuple-element.16.refs_1_, ...), custom_call_target="tpu_custom_call" | custom-call | tf_op jit(solution)/shard_map/pallas_call | solution.py:693

commit v8 on v7

--- a/solution.py
+++ b/solution.py
@@ -111,12 +111,12 @@
 
 
 def kernel(
-    ids_ref, live_ref, router_ref, tok_ref, og_ref, up_hbm, down_hbm,
+    ids_ref, live_ref, router_ref, tok_hbm, og_hbm, up_hbm, down_hbm,
     mixed_ref, tgrad_ref, upg_hbm, downg_hbm, rgrad_ref,
-    box, inz, outx, inx, ubox, uinz, uoutx, uinx, raw, yb, wu, wd, hid, dh, act, hc,
+    tok_ref, og_ref, box, inz, outx, inx, ubox, uinz, uoutx, uinx, raw, yb, wu, wd, hid, dh, act, hc,
     lg, gate_s, slope_s, slope3, sa, ra, sb, rb, ua, ub, gsu, gsd,
     p1, p1t, p2, p2t, plc, pltx, pltc, rrow, vt, vy, vx, vz,
-    wsem, zs, zr, xs, xr, ys, yr, as_, ar, bs, br, uzs, uzr, uxs, uxr, rs, rr,
+    tsem, wsem, zs, zr, xs, xr, ys, yr, as_, ar, bs, br, uzs, uzr, uxs, uxr, rs, rr,
     uas, uar, ubs, ubr, gsem, vts, vtr, vys, vyr, vxs, vxr, vzs, vzr, free,
 ):
     me = lax.axis_index("expert")
@@ -235,14 +235,23 @@
     def vzland(d):
         return remote(vx, vz.at[(z + NZ - d) % NZ], vzs.at[d], vzr.at[d], zpeer(d))
 
-    for s in range(NC):
-        for copy in weights(s):
-            copy.start()
+    rows_in = (
+        pltpu.make_async_copy(tok_hbm, tok_ref, tsem.at[0]),
+        pltpu.make_async_copy(og_hbm, og_ref, tsem.at[1]),
+    )
+    for copy in rows_in:
+        copy.start()
 
     barrier = pltpu.get_barrier_semaphore()
     for peers, ds in ((zpeer, ZD), (xpeer, XD), (ypeer, YD)):
         for d in ds:
             pl.semaphore_signal(barrier, inc=1, device_id=peers(d), device_id_type=MESH)
+
+    for s in range(NC):
+        for copy in weights(s):
+            copy.start()
+    for copy in rows_in:
+        copy.wait()
 
     diag = iota((ROWS, ROWS), 0) == iota((ROWS, ROWS), 1)
 
@@ -711,6 +720,8 @@
     every = NT * SLOTS
     V, DMA = pltpu.VMEM, pltpu.SemaphoreType.DMA
     scratch = [
+        V((ROWS, width), BF16),
+        V((ROWS, width), BF16),
         V((NN, NZ, ZR, C), BF16),
         V((NN, NZ, ZR, C), BF16),
         V((NN, NQ, XR, C), BF16),
@@ -751,6 +762,7 @@
         V((NT, 1, width), F32),
         V((NQ, 1, width), F32),
         V((NZ, NQ, 1, width), F32),
+        DMA((2,)),
         DMA((2, NC)),
         DMA((NN,)), DMA((NN,)), DMA((NN,)), DMA((NN,)), DMA((NN, 4)), DMA((NN, 4)),
         DMA((NN, 2)), DMA((NN, 2)), DMA((NN, 4)), DMA((NN, 4)),
@@ -771,7 +783,7 @@
             S((1, H, width), BF16),
             S((EXPERTS, width), F32),
         ),
-        in_specs=[vmem, smem, vmem, vmem, vmem, hbm, hbm],
+        in_specs=[vmem, smem, vmem, hbm, hbm, hbm, hbm],
         out_specs=(vmem, vmem, hbm, hbm, vmem),
         scratch_shapes=scratch,
         compiler_params=pltpu.CompilerParams(

time: 158 us -> 158 us (level)
  no operation moved by 1% of the time
where the time goes in v8:
time: 158 us
  Pallas kernels  156 us (99%)
    pallas_call x1, Pallas kernels, per_device(): pl.pallas_call(kernel, out_shape=(S((ROWS, width), BF16), S((ROWS, width)...  147 us
    pallas_call x1, Pallas kernels, hand_over(): pl.pallas_call(body, out_shape=tuple((jax.ShapeDtypeStruct(a.shape, a.dty...  8.89 us

profile of v8, /device:TPU:1, one launch (start us, length us, event | category | flops | bytes accessed | tf_op | source)
XLA Modules:
  0.0 157.5 jit_solution(12885627383407294889)
XLA Ops:
  1.3 147.4 %shard_map.110 = (bf16[128,2560]{1,0:T(8,128)(2,1)}, bf16[128,2560]{1,0:T(8,128)(2,1)}, bf16[1,2560,1024]{2,1,0:T(8,128)(2,1)}, bf16[1,1024,2560]{2,1,0:T(8,128)(2,1)}, f32[32,2560]{1,0:T(8,128)}) custom-call(s32[1,128]{1,0:T(1,128)} %bitcast.4, s32[1]{0:T(128)S(6)} %copy.12.live_ref, bf16[32,2560]{1,0:T(8,128)(2,1)} %bitcast.3, bf16[128,2560]{1,0:T(8,128)(2,1)} %tok_hbm.1, ...), custom_call_target="tpu_custom_call" | custom-call | tf_op jit(solution)/shard_map/pallas_call | solution.py:777
  148.6 8.9 %shard_map.111 = (bf16[128,2560]{1,0:T(8,128)(2,1)}, bf16[128,2560]{1,0:T(8,128)(2,1)}, bf16[1,2560,1024]{2,1,0:T(8,128)(2,1)}, bf16[1,1024,2560]{2,1,0:T(8,128)(2,1)}, f32[32,2560]{1,0:T(8,128)}) custom-call(bf16[128,2560]{1,0:T(8,128)(2,1)} %get-tuple-element.15.refs_0_, bf16[128,2560]{1,0:T(8,128)(2,1)} %get-tuple-element.16.refs_1_, ...), custom_call_target="tpu_custom_call" | custom-call | tf_op jit(solution)/shard_map/pallas_call | solution.py:702
